TPU v7x, 128 devices: a whole 4x4x4 slice. The times are simulated.
128 devices in a mesh: row: 8 (over y, z_hi), col: 16 (over z_lo, x, core).
Axes of the slice: x: 4, y: 4, z: 4 (z_hi: 2, z_lo: 2; z = z_hi * 2 + z_lo), core: 2. Of those that a mesh axis runs over, the one named last changes fastest.
Arguments:
- features: float32 [2, 128, 1024, 128], P(None, 'row', 'col'), may hold values from -6 to 6
- cotangent: float32 [2, 128, 1024, 128], P(None, 'row', 'col'), may hold values from -6 to 6
- conv_kernel: float32 [7, 7, 128], P(None, None, ('row', 'col')), may hold values from -0.875 to 0.875
- conv_bias: float32 [128], P(('row', 'col')), may hold values from -3 to 3
- norm_gain: float32 [128], P(('row', 'col')), may hold values from 0.1 to 1.9
- norm_shift: float32 [128], P(('row', 'col')), may hold values from -2 to 2
- w_in: float32 [128, 512], P(None, ('row', 'col')), may hold values from -0.5 to 0.5
- in_bias: float32 [512], P(('row', 'col')), may hold values from -3 to 3
- w_out: float32 [512, 128], P(('row', 'col')), may hold values from -0.25 to 0.25
- out_bias: float32 [128], P(('row', 'col')), may hold values from -3 to 3
- layer_scale: float32 [128], P(('row', 'col')), may hold values from 0.5 to 1.5
Outputs:
- features_grad: float32 [2, 128, 1024, 128], P(None, 'row', 'col')
- kernel_grad: float32 [7, 7, 128], P(None, None, ('row', 'col'))
- conv_bias_grad: float32 [128], P(('row', 'col'))
- gain_grad: float32 [128], P(('row', 'col'))
- shift_grad: float32 [128], P(('row', 'col'))
- w_in_grad: float32 [128, 512], P(None, ('row', 'col'))
- in_bias_grad: float32 [512], P(('row', 'col'))
- w_out_grad: float32 [512, 128], P(('row', 'col'))
- out_bias_grad: float32 [128], P(('row', 'col'))
- scale_grad: float32 [128], P(('row', 'col'))
All inputs are finite; a program needn't handle non-finite values.
Results may differ from a plain program's by a relative error of at most 0.0003.
Values sent between devices are 32-bit elements; how exact they have to be, the bound alone decides.
A program may use at most 64 MiB of HBM per device.

v0:
```python
import math

import jax
import jax.numpy as jnp
from jax import lax
from jax.sharding import PartitionSpec as P

norm_eps = 1e-06
inverse_root_two = 0.7071067811865476
inverse_root_twopi = 0.3989422804014327


def extended(block, sides, width):
    for axis, dim in sides:
        count = lax.axis_size(axis)
        forward = [(i, i + 1) for i in range(count - 1)]
        backward = [(target, source) for source, target in forward]
        low = lax.ppermute(
            lax.slice_in_dim(block, block.shape[dim] - width, None, axis=dim), axis, forward
        )
        high = lax.ppermute(lax.slice_in_dim(block, 0, width, axis=dim), axis, backward)
        block = jnp.concatenate([low, block, high], axis=dim)
    return block


def depthwise(field, kernel):
    return lax.conv_general_dilated(
        field,
        kernel[:, :, None, :],
        (1, 1),
        "VALID",
        dimension_numbers=("NHWC", "HWIO", "NHWC"),
        feature_group_count=field.shape[-1],
        precision=lax.Precision.HIGHEST,
    )


def cell_total(block):
    return jnp.sum(block, axis=(0, 1, 2))


def mixing_back(
    conv_out,
    cot_field,
    gain_all,
    shift_all,
    input_all,
    inbias_all,
    output_all,
    outbias_all,
    scale_all,
):
    highest = lax.Precision.HIGHEST
    mean = jnp.mean(conv_out, -1, keepdims=True)
    centred = conv_out - mean
    variance = jnp.mean(centred * centred, -1, keepdims=True)
    inverse = lax.rsqrt(variance + norm_eps)
    normed = centred * inverse
    lin = normed * gain_all + shift_all
    act = jnp.einsum("bhwc,ck->bhwk", lin, input_all, precision=highest) + inbias_all
    hidden = 0.5 * act * (1.0 + lax.erf(act * inverse_root_two))
    branch = jnp.einsum("bhwk,kc->bhwc", hidden, output_all, precision=highest) + outbias_all
    d_branch = cot_field * scale_all
    d_hidden = jnp.einsum("bhwc,kc->bhwk", d_branch, output_all, precision=highest)
    slope = (
        0.5 * (1.0 + lax.erf(act * inverse_root_two))
        + act * jnp.exp(-0.5 * act * act) * inverse_root_twopi
    )
    d_act = d_hidden * slope
    d_lin = jnp.einsum("bhwk,ck->bhwc", d_act, input_all, precision=highest)
    d_norm = d_lin * gain_all
    d_conv = inverse * (
        d_norm
        - jnp.mean(d_norm, -1, keepdims=True)
        - normed * jnp.mean(d_norm * normed, -1, keepdims=True)
    )
    gain_grad = cell_total(d_lin * normed)
    shift_grad = cell_total(d_lin)
    win_grad = jnp.einsum("bhwc,bhwk->ck", lin, d_act, precision=highest)
    inb_grad = cell_total(d_act)
    wout_grad = jnp.einsum("bhwk,bhwc->kc", hidden, d_branch, precision=highest)
    outb_grad = cell_total(d_branch)
    scale_grad = cell_total(cot_field * branch)
    return (d_conv, (gain_grad, shift_grad, win_grad, inb_grad, wout_grad, outb_grad, scale_grad))


def per_device(
    features,
    cotangent,
    conv_kernel,
    conv_bias,
    norm_gain,
    norm_shift,
    w_in,
    in_bias,
    w_out,
    out_bias,
    layer_scale,
):
    gathered = (
        lax.all_gather(conv_kernel, ("row", "col"), axis=2, tiled=True),
        lax.all_gather(conv_bias, ("row", "col"), axis=0, tiled=True),
        lax.all_gather(norm_gain, ("row", "col"), axis=0, tiled=True),
        lax.all_gather(norm_shift, ("row", "col"), axis=0, tiled=True),
        lax.all_gather(w_in, ("row", "col"), axis=1, tiled=True),
        lax.all_gather(in_bias, ("row", "col"), axis=0, tiled=True),
        lax.all_gather(w_out, ("row", "col"), axis=0, tiled=True),
        lax.all_gather(out_bias, ("row", "col"), axis=0, tiled=True),
        lax.all_gather(layer_scale, ("row", "col"), axis=0, tiled=True),
    )
    (
        kernel_all,
        conv_all,
        gain_all,
        shift_all,
        input_all,
        inbias_all,
        output_all,
        outbias_all,
        scale_all,
    ) = gathered
    margin = kernel_all.shape[0] // 2
    source = extended(features, (("row", 1), ("col", 2)), margin)
    conv_out = depthwise(source, kernel_all) + conv_all
    dconv_inner, partials = mixing_back(
        conv_out,
        cotangent,
        gain_all,
        shift_all,
        input_all,
        inbias_all,
        output_all,
        outbias_all,
        scale_all,
    )
    dconv_wide = extended(dconv_inner, (("row", 1), ("col", 2)), margin)
    features_grad = cotangent + depthwise(dconv_wide, kernel_all[::-1, ::-1])
    kernel_part = jax.vjp(lambda weights: depthwise(source, weights), kernel_all)[1](dconv_inner)[0]
    bias_part = jnp.sum(dconv_inner, axis=(0, 1, 2))
    cells = (
        features.shape[0]
        * features.shape[1]
        * features.shape[2]
        * lax.axis_size("row")
        * lax.axis_size("col")
    )
    factor = 1.0 / math.sqrt(cells)
    gain_p, shift_p, win_p, inb_p, wout_p, outb_p, scale_p = partials
    reduced = (
        lax.psum_scatter(kernel_part * factor, ("row", "col"), scatter_dimension=2, tiled=True),
        lax.psum_scatter(bias_part * factor, ("row", "col"), scatter_dimension=0, tiled=True),
        lax.psum_scatter(gain_p * factor, ("row", "col"), scatter_dimension=0, tiled=True),
        lax.psum_scatter(shift_p * factor, ("row", "col"), scatter_dimension=0, tiled=True),
        lax.psum_scatter(win_p * factor, ("row", "col"), scatter_dimension=1, tiled=True),
        lax.psum_scatter(inb_p * factor, ("row", "col"), scatter_dimension=0, tiled=True),
        lax.psum_scatter(wout_p * factor, ("row", "col"), scatter_dimension=0, tiled=True),
        lax.psum_scatter(outb_p * factor, ("row", "col"), scatter_dimension=0, tiled=True),
        lax.psum_scatter(scale_p * factor, ("row", "col"), scatter_dimension=0, tiled=True),
    )
    (
        kernel_grad,
        bias_grad,
        gain_grad,
        shift_grad,
        win_grad,
        inb_grad,
        wout_grad,
        outb_grad,
        scale_grad,
    ) = reduced
    return (
        features_grad,
        kernel_grad,
        bias_grad,
        gain_grad,
        shift_grad,
        win_grad,
        inb_grad,
        wout_grad,
        outb_grad,
        scale_grad,
    )


def solution(mesh):
    in_specs = (
        P(None, "row", "col", None),
        P(None, "row", "col", None),
        P(None, None, ("row", "col")),
        P(("row", "col")),
        P(("row", "col")),
        P(("row", "col")),
        P(None, ("row", "col")),
        P(("row", "col")),
        P(("row", "col"), None),
        P(("row", "col")),
        P(("row", "col")),
    )
    out_specs = (
        P(None, "row", "col", None),
        P(None, None, ("row", "col")),
        P(("row", "col")),
        P(("row", "col")),
        P(("row", "col")),
        P(None, ("row", "col")),
        P(("row", "col")),
        P(("row", "col"), None),
        P(("row", "col")),
        P(("row", "col")),
    )
    return jax.shard_map(
        per_device, mesh=mesh, in_specs=in_specs, out_specs=out_specs, check_vma=False
    )
```

profile of v0, /device:TPU:1, one launch (start us, length us, event | category | flops | bytes accessed | tf_op | source)
XLA Modules:
  0.0 425.7 jit_solution(4927064167426286075)
XLA Ops:
  7.2 1.1 fusion.55
  8.4 0.8 copy.127
  9.2 7.0 %collective-permute-start = (f32[2,3,64,128]{3,0,2,1:T(2,128)}, f32[2,3,64,128]{3,0,2,1:T(2,128)}, u32[]{:S(2)}, u32[]{:S(2)}) collective-permute-start(f32[2,3,64,128]{3,0,2,1:T(2,128)} %copy.127), channel_id=1, source_target_pairs={{0,16},{16,32},{32,48},{48,64},{64,80},{80,96},{96,112},{1,17},{17... | collective-permute-start | bytes 589832 | tf_op jit(solution)/shard_map/ppermute | solution.py:18
  16.2 0.8 copy.128
  17.0 1.3 collective-permute-start.1
  18.3 38.5 %all-gather.1 = f32[128,4,128]{2,1,0:T(4,128)S(1)} all-gather(f32[1,4,128]{2,1,0:T(4,128)} %bitcast.98), channel_id=1, replica_groups=mesh['row'=8,'col'=16] {'row','col'}, dimensions={0}, use_global_device_ids=true | all-gather | bytes 264192 | tf_op jit(solution)/shard_map/all_gather | solution.py:105
  60.1 0.7 copy.73
  60.8 33.9 %all_gather.27 = f32[7,7,128]{1,0,2:T(8,128)S(1)} all-gather(f32[7,7,1]{1,0,2:T(8,128)S(1)} %copy.73), channel_id=1, replica_groups=mesh['row'=8,'col'=16] {'row','col'}, dimensions={2}, use_global_device_ids=true | all-gather | bytes 25284 | tf_op jit(solution)/shard_map/all_gather | solution.py:101
  95.2 0.8 copy.93
  97.0 63.9 %all-reduce.16 = (f32[128]{0:T(128)S(1)}, f32[128]{0:T(128)S(1)}, f32[128]{0:T(128)}, f32[512]{0:T(512)}, f32[128]{0:T(128)S(1)}, /*index=5*/f32[128]{0:T(128)}) all-reduce(f32[128]{0:T(128)S(1)} %dynamic-update-slice.3, f32[128]{0:T(128)S(1)} %dynamic-update-slice.2, ...), channel_id=1, replica_groups=mesh['row'=8,'col'=16] {'row','col'}, use_global_device_ids=true, to_apply=%add.3 | all-reduce | flops 1152 | bytes 9216
  161.1 0.9 constant_dynamic-update-slice_fusion.2
  162.1 0.9 constant_dynamic-update-slice_fusion.1
  163.0 1.0 constant_dynamic-update-slice_fusion
  164.0 1.9 collective-permute-start.2
  165.9 2.4 collective-permute-start.3
  168.3 37.6 %all-gather = f32[128,4,128]{2,1,0:T(4,128)S(1)} all-gather(f32[1,4,128]{2,1,0:T(4,128)S(1)} %bitcast.99), channel_id=1, replica_groups=mesh['row'=8,'col'=16] {'row','col'}, dimensions={0}, use_global_device_ids=true | all-gather | bytes 264192 | tf_op jit(solution)/shard_map/all_gather | solution.py:107
  206.0 0.7 fusion.51
  208.1 5.9 %fusion.56 = (f32[16,16,9]{1,2,0:T(8,128)S(1)}, f32[16,16,9,128]{3,1,2,0:T(8,128)S(1)}) fusion(f32[128]{0:T(128)S(1)} %copy-done.15, f32[7,7,1,128]{3,2,1,0:T(1,128)S(1)} %copy-done.7, f32[22,2,7,6,128]{4,2,1,3,0:T(8,128)S(1)} %slice.41, f32[22,2,8,9,128]{4,2,1,3,0:T(8,128)S(1)} %copy.72, pred[16,9]{0,1:T(8,128)(4,1)S(1)} %copy-done.16), kind=kOutput, calls=%fused_computation.87 | convolution fusion | flops 176318208 | bytes 3782800 | tf_op jit(solution)/shard_map/conv_general_dilated | solution.py:27
  214.8 0.7 multiply_reduce_fusion.2
  215.6 3.6 fusion.34
  219.2 8.0 %fusion.30 = f32[512,128]{1,0:T(8,128)} fusion(f32[2,16,64,512]{3,2,1,0:T(8,128)S(1)} %fusion.34, f32[512]{0:T(512)S(1)} %copy-done.12, f32[2,16,64,128]{3,2,1,0:T(8,128)S(1)} %copy-done.1, f32[128]{0:T(128)S(1)} %copy-done.10), kind=kOutput, calls=%fused_computation.33 | convolution fusion | flops 1616183296 | bytes 5507584 | tf_op jit(solution)/shard_map/bhwk,bhwc->kc/dot_general | solution.py:81
  227.3 5.2 %fusion.57 = (f32[512]{0:T(512)S(1)}, f32[2,16,64,512]{3,2,1,0:T(8,128)S(1)}) fusion(f32[2,16,64,512]{3,2,1,0:T(8,128)S(1)} %fusion.34, f32[512]{0:T(512)S(1)} %copy-done.12, f32[512,128,1,1]{1,0,3,2:T(8,128)S(1)} %bitcast.96, f32[2,16,64,128]{3,2,1,0:T(8,128)S(1)} %copy-done.1, f32[128]{0:T(128)S(1)} %copy-done.10), kind=kOutput, calls=%fused_computation.88 | convolution fusion | flops 1622408704 | bytes 9703936 | tf_op jit(solution)/shard_map/bhwc,kc->bhwk/dot_general | solution.py:64
  232.4 2.0 copy-done
  234.4 8.2 %fusion.28 = f32[128,512]{0,1:T(8,128)} fusion(f32[2,16,64,512]{3,2,1,0:T(8,128)S(1)} %get-tuple-element.83, f32[128]{0:T(128)S(1)} %get-tuple-element.61, f32[128]{0:T(128)S(1)} %get-tuple-element.62, f32[16,2,64,128]{3,0,2,1:T(8,128)S(1)} %slice.42, f32[2,16,64]{2,1,0:T(8,128)S(1)} %add_rsqrt_fusion, f32[2,16,64]{2,1,0:T(8,128)S(1)} %copy.79), kind=kOutput, calls=%fused_computation.31 | convolution fusion | flops 1611726848 | bytes 5522432 | tf_op jit(solution)/shard_map/bhwc,bhwk->ck/dot_general | solution.py:79
  242.7 5.7 %multiply_reduce_fusion = (f32[128]{0:T(128)S(1)}, f32[2,16,64]{2,1,0:T(8,128)S(1)}, f32[2,16,64]{2,1,0:T(8,128)S(1)}, f32[128]{0:T(128)S(1)}, f32[2,16,64,128]{3,2,1,0:T(8,128)S(1)}) fusion(f32[2,16,64]{2,1,0:T(8,128)S(1)} %add_rsqrt_fusion, f32[2,16,64]{2,1,0:T(8,128)S(1)} %copy.79, f32[16,2,64,128]{3,0,2,1:T(8,128)S(1)} %slice.42, ...), kind=kOutput, calls=%fused_computation.40 | convolution fusion | flops 1612967680 | bytes 6587904 | tf_op jit(solution)/shard_map/bhwk,ck->bhwc/dot_general | solution.py:70
  248.4 4.1 fusion.27
  252.5 1.8 fusion.52
  254.3 3.1 collective-permute-start.4
  257.5 1.7 collective-permute-start.5
  259.2 21.3 %convolution_multiply_fusion = f32[7,7,1,128]{3,2,1,0:T(1,128)S(1)} fusion(f32[2,16,64,128]{3,2,1,0:T(8,128)S(1)} %get-tuple-element.70, f32[2,22,3,128]{3,0,2,1:T(2,128)} %copy-done.6, f32[2,22,64,128]{3,0,2,1:T(2,128)} %copy-done.4, f32[2,22,3,128]{3,0,2,1:T(2,128)S(1)} %collective-permute-done.2), kind=kOutput, calls=%fused_computation.34 | convolution fusion | flops 154935424 | bytes 2650624 | tf_op jit(solution)/shard_map/transpose(jvp())/conv_general_dilated | solution.py:27
  280.8 70.8 %all-reduce.15 = (f32[7,7,128]{1,0,2:T(8,128)}, f32[128]{0:T(128)S(1)}, f32[128]{0:T(128)S(1)}, f32[128]{0:T(128)S(1)}, f32[512]{0:T(512)S(1)}, /*index=5*/f32[128]{0:T(128)S(1)}, f32[128]{0:T(128)S(1)}) all-reduce(f32[7,7,128]{1,0,2:T(8,128)S(1)} %bitcast.94, ...), channel_id=2, replica_groups=mesh['row'=8,'col'=16] {'row','col'}, use_global_device_ids=true, to_apply=%region_4.0.clone | all-reduce | flops 7424 | bytes 59392
  351.6 0.6 dynamic-slice.8
  352.2 0.6 dynamic-slice.7
  352.8 0.6 dynamic-slice.3
  353.4 0.6 dynamic-slice.2
  354.0 0.6 dynamic-slice.1
  354.6 0.7 constant_dynamic-slice_fusion.2
  355.2 0.6 copy.88
  356.5 2.4 collective-permute-start.6
  358.9 2.1 collective-permute-start.7
  361.0 44.3 %all-reduce.20.cloned.1.call-done = (f32[128,512]{0,1:T(8,128)}, f32[512,128]{1,0:T(8,128)}) async-done(((f32[128,512]{0,1:T(8,128)}, f32[512,128]{1,0:T(8,128)}), (f32[128,512]{0,1:T(8,128)}, f32[512,128]{1,0:T(8,128)})) %all-reduce.20.cloned.1.call-update) | async-done | bytes 524304
  405.3 1.3 constant_dynamic-slice_fusion.1
  406.6 1.3 constant_dynamic-slice_fusion
  408.0 0.8 copy.96
  409.8 1.0 fusion.5
  410.8 5.4 %fusion.18 = f32[16,16,9,128]{3,1,2,0:T(8,128)S(1)} fusion(f32[7,7,1,128]{3,2,1,0:T(1,128)S(1)} %copy.82, f32[22,2,8,15,128]{4,1,3,2,0:T(2,128)S(1)} %fusion.5, pred[16,9]{0,1:T(8,128)(4,1)S(1)} %copy-done.17), kind=kOutput, calls=%fused_computation.26 | convolution fusion | flops 173703168 | bytes 3908240 | tf_op jit(solution)/shard_map/conv_general_dilated | solution.py:27
  416.7 0.6 fusion.31
  417.3 1.3 copy.87
  (85 shorter events, 6.3 us)
Async XLA Ops:
  7.2 89.5 %copy-start.13 = (f32[4]{0:T(128)S(1)}, f32[4]{0:T(128)}, u32[]{:S(2)}) copy-start(f32[4]{0:T(128)} %param.18) | copy-start | bytes 52
  7.2 153.6 %copy-start.1 = (f32[2,16,64,128]{3,2,1,0:T(8,128)S(1)}, f32[2,16,64,128]{3,2,1,0:T(8,128)}, u32[]{:S(2)}) copy-start(f32[2,16,64,128]{3,2,1,0:T(8,128)} %param.12) | copy-start | bytes 3145732
  7.2 398.1 %all-reduce.20.cloned.1.call-start = ((), (), s32[]{:S(2)}) async-start(), calls=%async_computation | async-start | bytes 1048576
  8.4 153.7 %copy-start.5 = (f32[2,16,64,128]{3,2,1,0:T(8,128)S(1)}, f32[2,16,64,128]{3,2,1,0:T(8,128)}, u32[]{:S(2)}) copy-start(f32[2,16,64,128]{3,2,1,0:T(8,128)} %param.11) | copy-start | bytes 3145732
  9.2 151.9 %collective-permute-start = (f32[2,3,64,128]{3,0,2,1:T(2,128)}, f32[2,3,64,128]{3,0,2,1:T(2,128)}, u32[]{:S(2)}, u32[]{:S(2)}) collective-permute-start(f32[2,3,64,128]{3,0,2,1:T(2,128)} %copy.127), channel_id=1, source_target_pairs={{0,16},{16,32},{32,48},{48,64},{64,80},{80,96},{96,112},{1,17},{17... | collective-permute-start | bytes 589832 | tf_op jit(solution)/shard_map/ppermute | solution.py:18
  17.0 145.9 %collective-permute-start.1 = (f32[2,3,64,128]{3,0,2,1:T(2,128)}, f32[2,3,64,128]{3,0,2,1:T(2,128)}, u32[]{:S(2)}, u32[]{:S(2)}) collective-permute-start(f32[2,3,64,128]{3,0,2,1:T(2,128)} %copy.128), channel_id=1, source_target_pairs={{16,0},{32,16},{48,32},{64,48},{80,64},{96,80},{112,96},{17,1},{33... | collective-permute-start | bytes 589832 | tf_op jit(solution)/shard_map/ppermute | solution.py:21
  95.2 73.2 %copy-start.8 = (f32[4,128]{1,0:T(4,128)S(1)}, f32[4,128]{1,0:T(4,128)}, u32[]{:S(2)}) copy-start(f32[4,128]{1,0:T(4,128)} %param.19) | copy-start | bytes 6148
  160.8 7.5 %copy-start.9 = (f32[128]{0:T(128)}, f32[128]{0:T(128)S(1)}, u32[]{:S(2)}) copy-start(f32[128]{0:T(128)S(1)} %get-tuple-element.65) | copy-start | bytes 1540
  163.9 43.4 %copy-start.4 = (f32[2,22,64,128]{3,0,2,1:T(2,128)}, f32[2,22,64,128]{3,0,2,1:T(2,128)S(1)}, u32[]{:S(2)}) copy-start(f32[2,22,64,128]{3,0,2,1:T(2,128)S(1)} %constant_dynamic-update-slice_fusion) | copy-start | bytes 4325380
  164.0 42.0 %collective-permute-start.2 = (f32[2,22,3,128]{3,0,2,1:T(2,128)S(1)}, f32[2,22,3,128]{3,0,2,1:T(2,128)S(1)}, u32[]{:S(2)}, u32[]{:S(2)}) collective-permute-start(f32[2,22,3,128]{3,0,2,1:T(2,128)S(1)} %get-tuple-element.73), channel_id=1, source_target_pairs={{0,1},{1,2},{2,3},{3,4},{4,5},{5,6},{6,7},{7,8},{8,9},{9,10},{10,1... | collective-permute-start | bytes 202760 | tf_op jit(solution)/shard_map/ppermute | solution.py:18
  165.9 40.1 %collective-permute-start.3 = (f32[2,22,3,128]{3,0,2,1:T(2,128)S(1)}, f32[2,22,3,128]{3,0,2,1:T(2,128)S(1)}, u32[]{:S(2)}, u32[]{:S(2)}) collective-permute-start(f32[2,22,3,128]{3,0,2,1:T(2,128)S(1)} %get-tuple-element.74), channel_id=1, source_target_pairs={{1,0},{2,1},{3,2},{4,3},{5,4},{6,5},{7,6},{8,7},{9,8},{10,9},{11,1... | collective-permute-start | bytes 202760 | tf_op jit(solution)/shard_map/ppermute | solution.py:21
  206.0 1.6 copy-start.6
  207.3 0.7 copy-start.7
  207.3 0.7 copy-start.15
  207.3 0.7 copy-start.16
  215.5 3.7 copy-start.10
  215.5 3.7 copy-start.12
  219.2 8.1 %copy-start.2 = (f32[2,16,64,512]{3,2,1,0:T(8,128)}, f32[2,16,64,512]{3,2,1,0:T(8,128)S(1)}, u32[]{:S(2)}) copy-start(f32[2,16,64,512]{3,2,1,0:T(8,128)S(1)} %fusion.34) | copy-start | bytes 12582916
  232.4 2.0 copy-start
  242.7 5.7 %copy-start.3 = (f32[2,16,64,512]{3,2,1,0:T(8,128)S(1)}, f32[2,16,64,512]{3,2,1,0:T(8,128)}, u32[]{:S(2)}) copy-start(f32[2,16,64,512]{3,2,1,0:T(8,128)} %copy-done.2) | copy-start | bytes 12582916
  242.7 5.7 %copy-start.14 = (f32[128]{0:T(128)S(1)}, f32[128]{0:T(128)}, u32[]{:S(2)}) copy-start(f32[128]{0:T(128)} %get-tuple-element.66) | copy-start | bytes 1540
  254.3 102.1 %collective-permute-start.4 = (f32[2,3,64,128]{3,2,1,0:T(8,128)S(1)}, f32[2,3,64,128]{3,2,1,0:T(8,128)S(1)}, u32[]{:S(2)}, u32[]{:S(2)}) collective-permute-start(f32[2,3,64,128]{3,2,1,0:T(8,128)S(1)} %get-tuple-element.75), channel_id=1, source_target_pairs={{0,16},{16,32},{32,48},{48,64},{64,80},{80,96},{96,112},{1,17},{17... | collective-permute-start | bytes 589832 | tf_op jit(solution)/shard_map/ppermute | solution.py:18
  257.5 99.0 %collective-permute-start.5 = (f32[2,3,64,128]{3,2,1,0:T(8,128)S(1)}, f32[2,3,64,128]{3,2,1,0:T(8,128)S(1)}, u32[]{:S(2)}, u32[]{:S(2)}) collective-permute-start(f32[2,3,64,128]{3,2,1,0:T(8,128)S(1)} %get-tuple-element.76), channel_id=1, source_target_pairs={{16,0},{32,16},{48,32},{64,48},{80,64},{96,80},{112,96},{17,1},{33... | collective-permute-start | bytes 589832 | tf_op jit(solution)/shard_map/ppermute | solution.py:21
  259.2 21.3 %copy-start.11 = (f32[128]{0:T(128)S(1)}, f32[128]{0:T(128)}, u32[]{:S(2)}) copy-start(f32[128]{0:T(128)} %get-tuple-element.69) | copy-start | bytes 1540
  356.5 51.4 %collective-permute-start.6 = (f32[2,22,3,128]{3,2,1,0:T(4,128)S(1)}, f32[2,22,3,128]{3,2,1,0:T(4,128)S(1)}, u32[]{:S(2)}, u32[]{:S(2)}) collective-permute-start(f32[2,22,3,128]{3,2,1,0:T(4,128)S(1)} %get-tuple-element.71), channel_id=1, source_target_pairs={{0,1},{1,2},{2,3},{3,4},{4,5},{5,6},{6,7},{7,8},{8,9},{9,10},{10,1... | collective-permute-start | bytes 202760 | tf_op jit(solution)/shard_map/ppermute | solution.py:18
  358.9 48.9 %collective-permute-start.7 = (f32[2,22,3,128]{3,2,1,0:T(4,128)S(1)}, f32[2,22,3,128]{3,2,1,0:T(4,128)S(1)}, u32[]{:S(2)}, u32[]{:S(2)}) collective-permute-start(f32[2,22,3,128]{3,2,1,0:T(4,128)S(1)} %get-tuple-element.72), channel_id=1, source_target_pairs={{1,0},{2,1},{3,2},{4,3},{5,4},{6,5},{7,6},{8,7},{9,8},{10,9},{11,1... | collective-permute-start | bytes 202760 | tf_op jit(solution)/shard_map/ppermute | solution.py:21
  409.8 1.1 copy-start.17
Sparse Core Ops, SparseCore 0:
  259.3 145.9 all-reduce.19
where the time goes:
time: 432 us; the launch traced here: 426 us
  blocking collectives  245 us (57%)
  matrix products  67.6 us (16%)
  waiting for transfers between devices  44.3 us (10%)
  local copies, waits for them, and re-layouts  23.5 us (5%)
  starting transfers between devices  22 us (5%)
  between operations  18.1 us (4%)
  other arithmetic  5.48 us (1%)
    unnamed x2, blocking collectives  135 us
    unnamed x2, waiting for transfers between devices  44.3 us
    all_gather x1, blocking collectives, per_device(): lax.all_gather(w_in, ('row', 'col'), axis=1, tiled=True)  38.5 us
    all_gather x1, blocking collectives, per_device(): lax.all_gather(w_out, ('row', 'col'), axis=0, tiled=True)  37.6 us
    all_gather x1, blocking collectives, per_device(): lax.all_gather(conv_kernel, ('row', 'col'), axis=2, tiled=True)  33.9 us
    conv_general_dilated x3, matrix products, depthwise(): lax.conv_general_dilated(field, kernel[:, :, None, :], (1, 1), 'VALID', d...  32.7 us
    unnamed x65, local copies, waits for them, and re-layouts  16.8 us
    ppermute x4, starting transfers between devices, extended(): lax.ppermute(lax.slice_in_dim(block, block.shape[dim] - width, None, axis...  14.4 us
  transfers between devices with their start and end apart: 9, of which 1 were waited for; matrix products, arithmetic and copies ran while one was open for 8% of the time, Pallas kernels for 0%

commit v1 on v0

v1 whole, which is shorter than its diff:
```python
import functools
import math

import jax
import jax.numpy as jnp
from jax import lax
from jax.experimental import pallas as pl
from jax.experimental.pallas import tpu as pltpu
from jax.sharding import PartitionSpec as P

norm_eps = 1e-06
inverse_root_two = 0.7071067811865476
inverse_root_twopi = 0.3989422804014327
MESH = pl.DeviceIdType.MESH
f32, bf16 = jnp.float32, jnp.bfloat16

K, R = 7, 3
C, HID = 128, 512
B, H, W = 2, 16, 64
LEFT = 8
WE = W + 2 * LEFT
HE = H + 2 * R
ROWS, COLS = 8, 16
CHUNK = 4
M = CHUNK * W
TAPS, CB, GAIN, SHIFT, OB, SCALE, IB = 0, 49, 50, 51, 52, 53, 54


def split(x):
    hi = x.astype(bf16)
    return hi, (x - hi.astype(f32)).astype(bf16)


def dot(a, b):
    return jnp.dot(a, b, preferred_element_type=f32)


def lanes(x, n, axis):
    return lax.broadcasted_iota(jnp.int32, (x, n), axis)


class Place:
    def __init__(self):
        self.row, self.col = lax.axis_index("row"), lax.axis_index("col")
        self.y = self.row // 2
        self.z = lax.rem(self.row, 2) * 2 + self.col // 8
        self.g = lax.rem(self.col, 8)
        self.x, self.core = self.g // 2, lax.rem(self.g, 2)
        self.index = self.row * COLS + self.col

    def in_group(self, off):
        other = lax.rem(self.g + off, 8)
        return other, (self.row, self.col // 8 * 8 + other)

    def along_z(self, off):
        other = lax.rem(self.z + off, 4)
        return other, (self.y * 2 + other // 2, lax.rem(other, 2) * 8 + self.g)

    def along_y(self, off):
        other = lax.rem(self.y + off, 4)
        return other, (other * 2 + lax.rem(self.row, 2), self.col)

    def sibling(self):
        return (self.row, self.col + 1 - 2 * self.core)

    def neighbour(self, dr, dc):
        return (lax.rem(self.row + dr + ROWS, ROWS), lax.rem(self.col + dc + COLS, COLS))


STEPS = [(-1, 0), (1, 0), (0, -1), (0, 1), (-1, -1), (-1, 1), (1, -1), (1, 1)]


def rows_of(step, base, sent):
    if step == 0:
        return pl.ds(base, H)
    if sent:
        return pl.ds(base, R) if step < 0 else pl.ds(base + H - R, R)
    return pl.ds(R + H, R) if step < 0 else pl.ds(0, R)


def cols_of(step, base, sent):
    if step == 0:
        return pl.ds(base, W)
    if sent:
        return pl.ds(base, LEFT) if step < 0 else pl.ds(base + W - LEFT, LEFT)
    return pl.ds(LEFT + W, LEFT) if step < 0 else pl.ds(0, LEFT)


def edge_copies(place, src, row0, col0, ext, send, recv):
    copies = []
    for n, (dr, dc) in enumerate(STEPS):
        copies.append(
            pltpu.make_async_remote_copy(
                src_ref=src.at[:, rows_of(dr, row0, True), cols_of(dc, col0, True), :],
                dst_ref=ext.at[:, rows_of(dr, R, False), cols_of(dc, LEFT, False), :],
                send_sem=send.at[n],
                recv_sem=recv.at[n],
                device_id=place.neighbour(dr, dc),
                device_id_type=MESH,
            )
        )
    return copies


def clear_outside(place, ext):
    @pl.when(place.row == 0)
    def _():
        ext[:, 0:R] = jnp.zeros((B, R, WE, C), f32)

    @pl.when(place.row == ROWS - 1)
    def _():
        ext[:, R + H :] = jnp.zeros((B, R, WE, C), f32)

    @pl.when(place.col == 0)
    def _():
        ext[:, :, 0:LEFT] = jnp.zeros((B, HE, LEFT, C), f32)

    @pl.when(place.col == COLS - 1)
    def _():
        ext[:, :, LEFT + W :] = jnp.zeros((B, HE, LEFT, C), f32)


def conv_tile(ext, taps, b, wb, flip):
    acc = [None] * H
    for j in range(K):
        tap = [taps[(K - 1 - i) * K + K - 1 - j] if flip else taps[i * K + j] for i in range(K)]
        for e in range(HE):
            x = ext[b, e, LEFT - R + 8 * wb + j : LEFT - R + 8 * wb + j + 8, :]
            for i in range(K):
                p = e - i
                if 0 <= p < H:
                    term = tap[i] * x
                    acc[p] = term if acc[p] is None else acc[p] + term
    return acc


def kernel_grad_tile(ext, dcv, kacc, b, wb):
    grads = [dcv[b, R + p, LEFT + 8 * wb : LEFT + 8 * wb + 8, :] for p in range(H)]
    for j in range(K):
        acc = [kacc[i * K + j] for i in range(K)]
        for e in range(HE):
            x = ext[b, e, LEFT - R + 8 * wb + j : LEFT - R + 8 * wb + j + 8, :]
            for i in range(K):
                p = e - i
                if 0 <= p < H:
                    acc[i] = acc[i] + grads[p] * x
        for i in range(K):
            kacc[i * K + j] = acc[i]


def kernel(
    feat, cot_hbm, small_in, weight_in,
    fg_out, small_out, weight_out,
    src, cot, dcv, mid, fg, sg, wg, taps,
    win2, winlo, wintop, wintlo, wot2, wotlo, bias_eff,
    nacc, macc, inbacc, kacc, cotacc, dbacc,
    wp, wcore, wa, wry, wb_, wrz, wc, wrx, sp, sry, sb, srz, sc, srx,
    local, out_sem, fsend, frecv, dsend, drecv, agsend, agrecv, rssend, rsrecv,
):
    place = Place()
    me = place.index

    own = [
        pltpu.make_async_copy(feat, src.at[:, pl.ds(R, H), pl.ds(LEFT, W), :], local.at[0]),
        pltpu.make_async_copy(cot_hbm, cot, local.at[1]),
        pltpu.make_async_copy(small_in, sg.at[pl.ds(me, 1)], local.at[2]),
        pltpu.make_async_copy(weight_in, wg.at[:, pl.ds(me, 1)], local.at[3]),
    ]
    for copy in own:
        copy.start()

    barrier = pltpu.get_barrier_semaphore()
    partners = [place.neighbour(dr, dc) for dr, dc in STEPS]
    partners += [place.in_group(off)[1] for off in range(1, 8)]
    partners += [place.along_z(off)[1] for off in range(1, 4)]
    partners += [place.along_y(off)[1] for off in range(1, 4)]
    for partner in partners:
        pl.semaphore_signal(barrier, inc=1, device_id=partner, device_id_type=MESH)
    pl.semaphore_wait(barrier, len(partners))

    def remote(s, d, sem, partner, send, recv):
        return pltpu.make_async_remote_copy(
            src_ref=s, dst_ref=d, send_sem=send.at[sem], recv_sem=recv.at[sem],
            device_id=partner, device_id_type=MESH,
        )

    s1 = [remote(small_in, sg.at[pl.ds(me, 1)], off - 1, place.in_group(off)[1], agsend, agrecv) for off in range(1, 8)]
    w1 = [remote(weight_in, wg.at[:, pl.ds(me, 1)], 13 + off - 1, place.in_group(off)[1], agsend, agrecv) for off in range(1, 8)]
    zs, ys = pl.ds(me // 8 * 8, 8), pl.ds(me // 32 * 32, 32)
    s2 = [remote(sg.at[zs], sg.at[zs], 7 + off - 1, place.along_z(off)[1], agsend, agrecv) for off in range(1, 4)]
    w2 = [remote(wg.at[:, zs], wg.at[:, zs], 20 + off - 1, place.along_z(off)[1], agsend, agrecv) for off in range(1, 4)]
    s3 = [remote(sg.at[ys], sg.at[ys], 10 + off - 1, place.along_y(off)[1], agsend, agrecv) for off in range(1, 4)]
    w3 = [remote(wg.at[:, ys], wg.at[:, ys], 23 + off - 1, place.along_y(off)[1], agsend, agrecv) for off in range(1, 4)]
    edges = edge_copies(place, feat, 0, 0, src, fsend, frecv)

    def start(copies):
        for copy in copies:
            copy.start()

    def arrive(copies):
        for copy in copies:
            copy.wait_recv()

    start(s1)
    start(w1)
    start(edges)
    own[2].wait()
    own[3].wait()
    arrive(s1)
    start(s2)
    arrive(w1)
    start(w2)

    kacc[...] = jnp.zeros_like(kacc)
    nacc[...] = jnp.zeros_like(nacc)
    macc[...] = jnp.zeros_like(macc)
    inbacc[...] = jnp.zeros_like(inbacc)
    cotacc[...] = jnp.zeros_like(cotacc)
    dbacc[...] = jnp.zeros_like(dbacc)

    arrive(s2)
    start(s3)
    arrive(w2)
    start(w3)
    arrive(s3)

    small = sg[...].reshape(128, C)
    small_t = small.T
    for n in range(K * K):
        taps[n] = jnp.broadcast_to(small_t[TAPS + n : TAPS + n + 1, :], (8, C))
    conv_bias = jnp.broadcast_to(small_t[CB : CB + 1, :], (8, C))
    gain_col, shift_col = small[:, GAIN : GAIN + 1], small[:, SHIFT : SHIFT + 1]
    scale_col, ob_col = small[:, SCALE : SCALE + 1], small[:, OB : OB + 1]

    own[0].wait()
    own[1].wait()
    arrive(edges)
    clear_outside(place, src)

    def conv_step(b, carry):
        for wb in range(W // 8):
            acc = conv_tile(src, taps, b, wb, False)
            for p in range(H):
                mid[b, p, 8 * wb : 8 * wb + 8, :] = acc[p] + conv_bias
        return carry

    lax.fori_loop(0, B, conv_step, 0)

    arrive(w3)
    win_t = wg[0].reshape(HID, C)
    wo_t = wg[1].reshape(HID, C).T
    win = win_t.T
    hi, lo = split(win * gain_col)
    win2[0:C, :] = hi
    win2[C:, :] = hi
    winlo[...] = lo
    gain_row = small_t[GAIN : GAIN + 1, :]
    hi, lo = split(win_t * gain_row)
    wintop[:, 0:C] = hi
    wintop[:, C:] = lo
    hi, lo = split(wo_t * scale_col)
    wot2[0:C, :] = hi
    wot2[C:, :] = hi
    wotlo[...] = lo
    unit, chan = lanes(C, HID, 1), lanes(C, HID, 0)
    bias_terms = win * shift_col
    for k in range(4):
        bias_terms = bias_terms + jnp.where(unit == 4 * chan + k, small[:, IB + k : IB + k + 1], 0.0)
    bias_eff[...] = jnp.sum(bias_terms, axis=0, keepdims=True)

    def mix(b, p0):
        x = mid[b, pl.ds(p0, CHUNK)].reshape(M, C)
        ct = cot[b, pl.ds(p0, CHUNK)].reshape(M, C)
        mean = jnp.mean(x, axis=-1, keepdims=True)
        cen = x - mean
        inv = lax.rsqrt(jnp.mean(cen * cen, axis=-1, keepdims=True) + norm_eps)
        normed = cen * inv
        n_hi, n_lo = split(normed)
        n2 = jnp.concatenate([n_hi, n_lo], axis=1)
        c_hi, c_lo = split(ct)
        c2 = jnp.concatenate([c_hi, c_lo], axis=1)
        nt2 = jnp.concatenate(split(normed.T), axis=0)
        ct2 = jnp.concatenate(split(ct.T), axis=0)
        cotacc[...] += jnp.sum(ct.reshape(M // 8, 8, C), axis=0)
        dn = jnp.zeros((M, C), f32)
        step = 256
        for h in range(0, HID, step):
            cut = slice(h, h + step)
            act = dot(n2, win2[:, cut]) + dot(n_hi, winlo[:, cut]) + bias_eff[:, cut]
            dh = dot(c2, wot2[:, cut]) + dot(c_hi, wotlo[:, cut])
            phi = 0.5 * (1.0 + lax.erf(act * inverse_root_two))
            slope = phi + act * jnp.exp(-0.5 * act * act) * inverse_root_twopi
            hid_hi, hid_lo = split(act * phi)
            da = dh * slope
            inbacc[:, cut] += jnp.sum(da.reshape(M // 8, 8, step), axis=0)
            da_hi, da_lo = split(da)
            both = dot(da_hi, wintop[cut, :])
            dn = dn + both[:, 0:C] + both[:, C:] + dot(da_lo, wintop[cut, 0:C])
            both = dot(nt2, da_hi)
            nacc[:, cut] += both[0:C] + both[C:] + dot(nt2[0:C], da_lo)
            both = dot(ct2, hid_hi)
            macc[:, cut] += both[0:C] + both[C:] + dot(ct2[0:C], hid_lo)
        dc = inv * (
            dn
            - jnp.mean(dn, axis=-1, keepdims=True)
            - normed * jnp.mean(dn * normed, axis=-1, keepdims=True)
        )
        dbacc[...] += jnp.sum(dc.reshape(M // 8, 8, C), axis=0)
        dcv[b, pl.ds(R + p0, CHUNK), pl.ds(LEFT, W), :] = dc.reshape(CHUNK, W, C)

    def edge_step(n, carry):
        mix(n // 2, lax.rem(n, 2) * (H - CHUNK))
        return carry

    def inner_step(n, carry):
        mix(n // 2, CHUNK + lax.rem(n, 2) * CHUNK)
        return carry

    lax.fori_loop(0, 4, edge_step, 0)
    back = edge_copies(place, dcv, R, LEFT, dcv, dsend, drecv)
    start(back[0:2] + back[4:])
    lax.fori_loop(0, 4, inner_step, 0)
    start(back[2:4])

    factor = 1.0 / math.sqrt(B * H * W * ROWS * COLS)
    nsum, msum = nacc[...], macc[...]
    inb = jnp.sum(inbacc[...], axis=0, keepdims=True)
    wp[0] = ((nsum * gain_col + shift_col * inb) * factor).T
    wp[1] = (msum * (scale_col * factor)).T
    other = 1 - place.core
    r0 = remote(wp.at[other], wcore, 0, place.sibling(), rssend, rsrecv)
    r0.start()

    gain_g = jnp.sum(win * nsum, axis=1, keepdims=True)
    shift_g = jnp.sum(win * inb, axis=1, keepdims=True)
    scale_g = jnp.sum(wo_t * msum, axis=1, keepdims=True)
    inb_g = [jnp.sum(jnp.where(unit == 4 * chan + k, inb, 0.0), axis=1, keepdims=True) for k in range(4)]

    def kgrad_step(b, carry):
        for wb in range(W // 8):
            kernel_grad_tile(src, dcv, kacc, b, wb)
        return carry

    lax.fori_loop(0, 1, kgrad_step, 0)
    r0.wait_recv()
    wa[...] = wp[place.core] + wcore[...]
    r1 = []
    for off in range(1, 4):
        y, partner = place.along_y(off)
        r1.append(remote(wa.at[pl.ds(y * 128, 128)], wry.at[off - 1], off, partner, rssend, rsrecv))
    start(r1)
    lax.fori_loop(1, 2, kgrad_step, 0)

    for n in range(K * K):
        sc[n : n + 1, :] = jnp.sum(kacc[n], axis=0, keepdims=True)
    sc[K * K : K * K + 1, :] = jnp.sum(dbacc[...], axis=0, keepdims=True)
    sc[K * K + 1 :, :] = jnp.zeros((128 - K * K - 1, C), f32)
    grads = sc[...].T
    lane = lanes(C, 128, 1)
    cot_col = jnp.sum(cotacc[...], axis=0, keepdims=True)
    cot_col = jnp.broadcast_to(cot_col, (128, C)).T[:, 0:1]
    columns = [(GAIN, gain_g), (SHIFT, shift_g), (OB, scale_col * cot_col), (SCALE, scale_g + ob_col * cot_col)]
    columns += [(IB + k, inb_g[k]) for k in range(4)]
    for at, column in columns:
        grads = jnp.where(lane == at, column, grads)
    sp[...] = grads * factor
    q1 = []
    for off in range(1, 4):
        y, partner = place.along_y(off)
        q1.append(remote(sp.at[pl.ds(y * 32, 32)], sry.at[off - 1], 14 + off - 1, partner, rssend, rsrecv))
    start(q1)

    arrive(r1)
    wb_[...] = wa[pl.ds(place.y * 128, 128)] + wry[0] + wry[1] + wry[2]
    r2 = []
    for off in range(1, 4):
        z, partner = place.along_z(off)
        r2.append(remote(wb_.at[pl.ds(z * 32, 32)], wrz.at[off - 1], 4 + off - 1, partner, rssend, rsrecv))
    start(r2)
    arrive(q1)
    sb[...] = sp[pl.ds(place.y * 32, 32)] + sry[0] + sry[1] + sry[2]
    q2 = []
    for off in range(1, 4):
        z, partner = place.along_z(off)
        q2.append(remote(sb.at[pl.ds(z * 8, 8)], srz.at[off - 1], 17 + off - 1, partner, rssend, rsrecv))
    start(q2)

    arrive(back)
    clear_outside(place, dcv)

    def out_step(b, carry):
        for wb in range(W // 8):
            acc = conv_tile(dcv, taps, b, wb, True)
            for p in range(H):
                at = slice(8 * wb, 8 * wb + 8)
                fg[b, p, at, :] = acc[p] + cot[b, p, at, :]
        return carry

    lax.fori_loop(0, 1, out_step, 0)
    put0 = pltpu.make_async_copy(fg.at[0], fg_out.at[0], out_sem.at[0])
    put0.start()

    arrive(r2)
    wc[...] = wb_[pl.ds(place.z * 32, 32)] + wrz[0] + wrz[1] + wrz[2]
    r3 = []
    for off in range(1, 8):
        g, partner = place.in_group(off)
        r3.append(
            remote(wc.at[pl.ds(g // 2 * 8, 8)], wrx.at[place.core, place.x], 7 + off - 1, partner, rssend, rsrecv)
        )
    start(r3)
    wrx[place.core, place.x] = wc[pl.ds(place.x * 8, 8)]
    arrive(q2)
    srx[0] = sb[pl.ds(place.z * 8, 8)] + srz[0] + srz[1] + srz[2]
    q3 = []
    for off in range(1, 8):
        q3.append(remote(srx.at[0], srx.at[off], 20 + off - 1, place.in_group(off)[1], rssend, rsrecv))
    start(q3)

    lax.fori_loop(1, 2, out_step, 0)
    put1 = pltpu.make_async_copy(fg.at[1], fg_out.at[1], out_sem.at[1])
    put1.start()

    arrive(r3)
    for kind in range(2):
        total = wrx[kind, 0] + wrx[kind, 1] + wrx[kind, 2] + wrx[kind, 3]
        weight_out[kind] = jnp.where(place.core == 0, total[0:4], total[4:8])
    arrive(q3)
    total = srx[0]
    for off in range(1, 8):
        total = total + srx[off]
    mine = lanes(8, C, 0) == place.g
    small_out[...] = jnp.sum(jnp.where(mine, total, 0.0), axis=0, keepdims=True)

    put0.wait()
    put1.wait()
    for copy in s1 + w1 + s2 + w2 + s3 + w3 + edges + back + [r0] + r1 + r2 + r3 + q1 + q2 + q3:
        copy.wait_send()


def call(features, cotangent, small, weights):
    vmem = lambda *shape: pltpu.VMEM(shape, f32)
    half = lambda *shape: pltpu.VMEM(shape, bf16)
    dma = lambda n: pltpu.SemaphoreType.DMA((n,))
    anywhere = pl.BlockSpec(memory_space=pl.ANY)
    inside = pl.BlockSpec(memory_space=pltpu.VMEM)
    return pl.pallas_call(
        kernel,
        out_shape=(
            jax.ShapeDtypeStruct((B, H, W, C), f32),
            jax.ShapeDtypeStruct((1, C), f32),
            jax.ShapeDtypeStruct((2, 4, C), f32),
        ),
        in_specs=[anywhere, anywhere, inside, inside],
        out_specs=(anywhere, inside, inside),
        scratch_shapes=[
            vmem(B, HE, WE, C), vmem(B, H, W, C), vmem(B, HE, WE, C), vmem(B, H, W, C), vmem(B, H, W, C),
            vmem(128, 1, C), vmem(2, 128, 4, C), vmem(K * K, 8, C),
            half(2 * C, HID), half(C, HID), half(HID, 2 * C), half(8, C), half(2 * C, HID), half(C, HID), vmem(1, HID),
            vmem(C, HID), vmem(C, HID), vmem(8, HID), vmem(K * K, 8, C), vmem(8, C), vmem(8, C),
            vmem(2, HID, C), vmem(HID, C), vmem(HID, C), vmem(3, 128, C), vmem(128, C), vmem(3, 32, C), vmem(32, C),
            vmem(2, 4, 8, C), vmem(128, C), vmem(3, 32, C), vmem(32, C), vmem(3, 8, C), vmem(128, C), vmem(8, 8, C),
            dma(4), dma(2), dma(8), dma(8), dma(8), dma(8), dma(26), dma(26), dma(27), dma(27),
        ],
        compiler_params=pltpu.CompilerParams(
            collective_id=0, has_side_effects=True, vmem_limit_bytes=56 * 2**20
        ),
    )(features, cotangent, small, weights)


def per_device(
    features, cotangent, conv_kernel, conv_bias, norm_gain, norm_shift,
    w_in, in_bias, w_out, out_bias, layer_scale,
):
    small = jnp.concatenate(
        [
            conv_kernel.reshape(K * K), conv_bias, norm_gain, norm_shift, out_bias, layer_scale,
            in_bias, jnp.zeros((128 - IB - 4,), f32),
        ]
    ).reshape(1, 1, C)
    weights = jnp.stack([w_in.T, w_out]).reshape(2, 1, 4, C)
    fg, small_g, weight_g = call(features, cotangent, small, weights)
    row = small_g[0]
    return (
        fg,
        row[0 : K * K].reshape(K, K, 1),
        row[CB : CB + 1],
        row[GAIN : GAIN + 1],
        row[SHIFT : SHIFT + 1],
        weight_g[0].T,
        row[IB : IB + 4],
        weight_g[1],
        row[OB : OB + 1],
        row[SCALE : SCALE + 1],
    )


def solution(mesh):
    both = ("row", "col")
    tile = P(None, "row", "col", None)
    taps, vector = P(None, None, both), P(both)
    return jax.shard_map(
        per_device,
        mesh=mesh,
        in_specs=(tile, tile, taps, vector, vector, vector, P(None, both), vector, P(both, None), vector, vector),
        out_specs=(tile, taps, vector, vector, vector, P(None, both), vector, P(both, None), vector, vector),
        check_vma=False,
    )
```

time: 432 us -> 73 us (0.17); the launches traced: 426 us -> 72.7 us
  blocking collectives: 245 us -> 0 us
  matrix products: 67.6 us -> 0 us
  Pallas kernels: 0 us -> 61.3 us
  waiting for transfers between devices: 44.3 us -> 0 us
  starting transfers between devices: 22 us -> 0 us
  local copies, waits for them, and re-layouts: 23.5 us -> 6.85 us
  between operations: 18.1 us -> 3.93 us
  other arithmetic: 5.48 us -> 0.61 us
    unnamed x2 -> x0, blocking collectives: 135 us -> none
    all_gather x3 -> x0, blocking collectives: 110 us -> none  [the longest x1 38.5 us: per_device(): lax.all_gather(w_in, ('row', 'col'), axis=1, tiled=True)]
    pallas_call x0 -> x1, Pallas kernels: none -> 61.3 us  [call(): pl.pallas_call(kernel, out_shape=(jax.ShapeDtypeStruct((B, H, W, C), f32)...]
    unnamed x2 -> x0, waiting for transfers between devices: 44.3 us -> none
    dot_general x6 -> x0, matrix products: 34.9 us -> none  [the longest x1 8.25 us: mixing_back(): win_grad = jnp.einsum('bhwc,bhwk->ck', lin, d_act, precision=highest)]
    conv_general_dilated x3 -> x0, matrix products: 32.7 us -> none  [depthwise(): lax.conv_general_dilated(field, kernel[:, :, None, :], (1, 1), 'VALID', d...]
    ppermute x8 -> x0, starting transfers between devices: 22 us -> none  [the longest x4 14.4 us: extended(): lax.ppermute(lax.slice_in_dim(block, block.shape[dim] - width, None, axis...]
    unnamed x65 -> x13, local copies, waits for them, and re-layouts: 16.8 us -> 3.73 us
  transfers between devices with their start and end apart: 9 -> 0, of which waited for: 1 -> 0; matrix products, arithmetic and copies ran while one was open for 8% -> 0% of each run, Pallas kernels for 0% -> 0%
where the time goes in v1:
time: 73 us; the launch traced here: 72.7 us
  Pallas kernels  61.3 us (84%)
  local copies, waits for them, and re-layouts  6.85 us (9%)
  between operations  3.93 us (5%)
    pallas_call x1, Pallas kernels, call(): pl.pallas_call(kernel, out_shape=(jax.ShapeDtypeStruct((B, H, W, C), f32)...  61.3 us
    unnamed x13, local copies, waits for them, and re-layouts  3.73 us

profile of v1, /device:TPU:1, one launch (start us, length us, event | category | flops | bytes accessed | tf_op | source)
XLA Modules:
  0.0 72.7 jit_solution(14895490992440373305)
XLA Ops:
  2.6 0.0 copy-start.2
  3.9 0.0 copy-done.2
  3.9 0.1 reshape.40
  4.0 0.0 copy-start.5
  4.0 0.7 copy-done.5
  4.7 0.0 copy-start.3
  4.7 0.0 copy-start.4
  4.7 0.6 concatenate.3
  5.3 0.1 copy-done.3
  5.3 0.0 copy-done.4
  5.4 0.6 maximum_bitcast_fusion.weight_in
  6.0 61.3 %shard_map.186 = (f32[2,16,64,128]{3,2,1,0:T(8,128)}, f32[1,128]{1,0:T(1,128)}, f32[2,4,128]{2,1,0:T(4,128)}) custom-call(f32[2,16,64,128]{3,2,1,0:T(8,128)} %feat.1, f32[2,16,64,128]{3,2,1,0:T(8,128)} %cot_hbm.1, f32[1,1,128]{2,1,0:T(1,128)} %bitcast.20, f32[2,1,4,128]{3,2,1,0:T(4,128)} %maximum_bitcast_fusion.weight_in), custom_call_target="tpu_custom_call" | custom-call | tf_op jit(solution)/shard_map/pallas_call | solution.py:447
  67.3 0.0 copy-start
  67.3 0.7 copy-done
  67.9 0.6 slice_bitcast_fusion.2
  68.5 0.6 fusion
  69.1 0.0 copy-start.1
  69.1 0.7 reshape.44
  69.8 0.0 copy-done.1
  69.8 0.6 slice_bitcast_fusion
  70.4 2.3 %copy.29 = f32[2,16,64,128]{3,2,1,0:T(8,128)} copy(f32[2,16,64,128]{3,2,1,0:T(8,128)} %get-tuple-element.53) | data formatting | bytes 2097152
  (3 shorter events, 0.0 us)
Async XLA Ops:
  2.6 1.3 %copy-start.2 = (f32[7,7,1]{1,2,0:T(1,128)S(1)}, f32[7,7,1]{1,2,0:T(1,128)}, u32[]{:S(2)}) copy-start(f32[7,7,1]{1,2,0:T(1,128)} %param.13) | copy-start | bytes 592
  4.0 0.7 copy-start.5
  4.7 0.7 copy-start.3
  4.7 0.7 copy-start.4
  67.3 0.7 copy-start
  69.1 0.7 copy-start.1

commit v2 on v1

v2 whole, which is shorter than its diff:
```python
import functools
import math

import jax
import jax.numpy as jnp
from jax import lax
from jax.experimental import pallas as pl
from jax.experimental.pallas import tpu as pltpu
from jax.sharding import PartitionSpec as P

norm_eps = 1e-06
inverse_root_two = 0.7071067811865476
inverse_root_twopi = 0.3989422804014327
MESH = pl.DeviceIdType.MESH
f32, bf16 = jnp.float32, jnp.bfloat16

K, R = 7, 3
C, HID = 128, 512
B, H, W = 2, 16, 64
LEFT = 8
WE = W + 2 * LEFT
HE = H + 2 * R
ROWS, COLS = 8, 16
QUARTER = H // 4
M = 2 * QUARTER * W
TAPS, CB, GAIN, SHIFT, OB, SCALE, IB = 0, 49, 50, 51, 52, 53, 54


def split(x):
    hi = x.astype(bf16)
    return hi, (x - hi.astype(f32)).astype(bf16)


def dot(a, b):
    return jnp.dot(a, b, preferred_element_type=f32)


def lanes(x, n, axis):
    return lax.broadcasted_iota(jnp.int32, (x, n), axis)


class Place:
    def __init__(self):
        self.row, self.col = lax.axis_index("row"), lax.axis_index("col")
        self.y = self.row // 2
        self.z = lax.rem(self.row, 2) * 2 + self.col // 8
        self.g = lax.rem(self.col, 8)
        self.x, self.core = self.g // 2, lax.rem(self.g, 2)

    def at(self, y, z, x, core):
        return (y * 2 + z // 2, lax.rem(z, 2) * 8 + x * 2 + core)

    def turn(self, y=0, z=0, x=0):
        y, z, x = lax.rem(self.y + y, 4), lax.rem(self.z + z, 4), lax.rem(self.x + x, 4)
        return y, z, x, self.at(y, z, x, self.core)

    def in_plane(self, off):
        other = lax.rem(self.g + off, 8)
        return self.at(self.y, self.z, other // 2, lax.rem(other, 2))

    def in_column(self, off):
        other = lax.rem(self.z * 2 + self.core + off, 8)
        return self.at(self.y, other // 2, self.x, lax.rem(other, 2))

    def sibling(self):
        return self.at(self.y, self.z, self.x, 1 - self.core)

    def neighbour(self, dr, dc):
        return (lax.rem(self.row + dr + ROWS, ROWS), lax.rem(self.col + dc + COLS, COLS))


STEPS = [(0, -1), (0, 1), (-1, 0), (1, 0), (-1, -1), (-1, 1), (1, -1), (1, 1)]


def rows_of(step, base, sent):
    if step == 0:
        return pl.ds(base, H)
    if sent:
        return pl.ds(base, R) if step < 0 else pl.ds(base + H - R, R)
    return pl.ds(R + H, R) if step < 0 else pl.ds(0, R)


def cols_of(step, base, sent):
    if step == 0:
        return pl.ds(base, W)
    if sent:
        return pl.ds(base, LEFT) if step < 0 else pl.ds(base + W - LEFT, LEFT)
    return pl.ds(LEFT + W, LEFT) if step < 0 else pl.ds(0, LEFT)


def edge_copies(place, src, row0, col0, ext, send, recv):
    copies = []
    for n, (dr, dc) in enumerate(STEPS):
        copies.append(
            pltpu.make_async_remote_copy(
                src_ref=src.at[:, rows_of(dr, row0, True), cols_of(dc, col0, True), :],
                dst_ref=ext.at[:, rows_of(dr, R, False), cols_of(dc, LEFT, False), :],
                send_sem=send.at[n],
                recv_sem=recv.at[n],
                device_id=place.neighbour(dr, dc),
                device_id_type=MESH,
            )
        )
    return copies


def clear_columns(place, ext):
    @pl.when(place.col == 0)
    def _():
        ext[:, R : R + H, 0:LEFT] = jnp.zeros((B, H, LEFT, C), f32)

    @pl.when(place.col == COLS - 1)
    def _():
        ext[:, R : R + H, LEFT + W :] = jnp.zeros((B, H, LEFT, C), f32)


def clear_rows(place, ext):
    for edge, at in ((0, slice(0, R)), (ROWS - 1, slice(R + H, HE))):

        @pl.when(place.row == edge)
        def _():
            ext[:, at] = jnp.zeros((B, R, WE, C), f32)

        @pl.when(place.col == 0)
        def _():
            ext[:, at, 0:LEFT] = jnp.zeros((B, R, LEFT, C), f32)

        @pl.when(place.col == COLS - 1)
        def _():
            ext[:, at, LEFT + W :] = jnp.zeros((B, R, LEFT, C), f32)


def conv_tile(ext, taps, b, wb, flip, rows, acc):
    for j in range(K):
        tap = [taps[(K - 1 - i) * K + K - 1 - j] if flip else taps[i * K + j] for i in range(K)]
        for e in rows:
            x = ext[b, e, LEFT - R + 8 * wb + j : LEFT - R + 8 * wb + j + 8, :]
            for i in range(K):
                p = e - i
                if 0 <= p < H:
                    acc[p] = acc[p] + tap[i] * x
    return acc


INNER = range(R, R + H)
OUTER = (*range(R), *range(R + H, HE))
FRINGE = (*range(R), *range(H - R, H))


def kernel_grad_tile(ext, dcv, kacc, b, wb):
    grads = [dcv[b, R + p, LEFT + 8 * wb : LEFT + 8 * wb + 8, :] for p in range(H)]
    for j in range(K):
        acc = [kacc[i * K + j] for i in range(K)]
        for e in range(HE):
            x = ext[b, e, LEFT - R + 8 * wb + j : LEFT - R + 8 * wb + j + 8, :]
            for i in range(K):
                p = e - i
                if 0 <= p < H:
                    acc[i] = acc[i] + grads[p] * x
        for i in range(K):
            kacc[i * K + j] = acc[i]


def widen(column, n):
    one = jnp.broadcast_to(column, (column.shape[0], 128))
    return jnp.concatenate([one] * n, axis=1)


def kernel(
    feat, cot_hbm, taps_in, cb_in, gain_in, shift_in, ob_in, scale_in, ib_in, win_in, wout_in,
    fg_out, small_out, weight_out,
    taps_s, cb_s, gain_s, shift_s, ob_s, scale_s, ib_s, srow,
    src, cot, dcv, mid, fg, sg, wg, taps,
    win2, winlo, wintop, wot2, wotlo, bias_eff,
    nacc, macc, inbacc, kacc, cotacc, dbacc,
    wp, wcore, wa, wr1, wb_, wr2, wc, wr3, wd, wr4, rows, sp, sry, sb, srz, srx,
    local, out_sem, fsend, frecv, dsend, drecv, agsend, agrecv, rssend, rsrecv,
):
    place = Place()
    y, z, x, core = place.y, place.z, place.x, place.core

    scalars = [(taps_in, taps_s), (cb_in, cb_s), (gain_in, gain_s), (shift_in, shift_s), (ob_in, ob_s), (scale_in, scale_s), (ib_in, ib_s)]
    params = [pltpu.make_async_copy(a, b, local.at[4 + n]) for n, (a, b) in enumerate(scalars)]
    own = [
        pltpu.make_async_copy(feat, src.at[:, pl.ds(R, H), pl.ds(LEFT, W), :], local.at[0]),
        pltpu.make_async_copy(cot_hbm, cot, local.at[1]),
        pltpu.make_async_copy(win_in, wg.at[0, y, z, x, core], local.at[2]),
        pltpu.make_async_copy(wout_in, wg.at[1, y, z, x, core], local.at[3]),
    ]
    for copy in params + own:
        copy.start()

    barrier = pltpu.get_barrier_semaphore()
    partners = [place.neighbour(dr, dc) for dr, dc in STEPS]
    partners += [place.in_plane(off) for off in range(1, 8)]
    partners += [place.in_column(off) for off in range(1, 8)]
    partners += [place.turn(y=off)[3] for off in range(1, 4)]
    for partner in partners:
        pl.semaphore_signal(barrier, inc=1, device_id=partner, device_id_type=MESH)

    for copy in params:
        copy.wait()
    lane = lanes(1, 128, 1)
    row = jnp.zeros((1, 128), f32)
    for i in range(K):
        for j in range(K):
            row = jnp.where(lane == TAPS + i * K + j, taps_s[i, 0, j], row)
    for at, ref in ((CB, cb_s), (GAIN, gain_s), (SHIFT, shift_s), (OB, ob_s), (SCALE, scale_s)):
        row = jnp.where(lane == at, ref[0], row)
    for k in range(4):
        row = jnp.where(lane == IB + k, ib_s[k], row)
    srow[...] = row
    sg[y, z, x, core] = row
    kacc[...] = jnp.zeros_like(kacc)
    nacc[...] = jnp.zeros_like(nacc)
    macc[...] = jnp.zeros_like(macc)
    inbacc[...] = jnp.zeros_like(inbacc)
    cotacc[...] = jnp.zeros_like(cotacc)
    dbacc[...] = jnp.zeros_like(dbacc)

    pl.semaphore_wait(barrier, len(partners))

    def remote(s, d, sem, partner, send, recv):
        return pltpu.make_async_remote_copy(
            src_ref=s, dst_ref=d, send_sem=send.at[sem], recv_sem=recv.at[sem],
            device_id=partner, device_id_type=MESH,
        )

    def same(ref, sem, partner):
        return remote(ref, ref, sem, partner, agsend, agrecv)

    cell = (y, z, x, core)
    group = [place.in_column(off) for off in range(1, 8)]
    xs = [place.turn(x=off)[3] for off in range(1, 4)]
    ys = [place.turn(y=off)[3] for off in range(1, 4)]
    s1 = [remote(srow, sg.at[cell], n, p, agsend, agrecv) for n, p in enumerate(group)]
    w1 = [remote(win_in, wg.at[(0, *cell)], 7 + n, p, agsend, agrecv) for n, p in enumerate(group)]
    v1 = [remote(wout_in, wg.at[(1, *cell)], 14 + n, p, agsend, agrecv) for n, p in enumerate(group)]
    s2 = [same(sg.at[y, :, x], 21 + n, p) for n, p in enumerate(xs)]
    w2 = [same(wg.at[0, y, :, x], 24 + n, p) for n, p in enumerate(xs)]
    v2 = [same(wg.at[1, y, :, x], 27 + n, p) for n, p in enumerate(ys)]
    s3 = [same(sg.at[y], 30 + n, p) for n, p in enumerate(ys)]
    w3 = [same(wg.at[0, y], 33 + n, p) for n, p in enumerate(ys)]
    v3 = [same(wg.at[1, :, :, x], 36 + n, p) for n, p in enumerate(xs)]
    edges = edge_copies(place, feat, 0, 0, src, fsend, frecv)

    def start(copies):
        for copy in copies:
            copy.start()

    def arrive(copies):
        for copy in copies:
            copy.wait_recv()

    start(s1)
    start(w1)
    start(v1)
    start(edges)
    own[2].wait()
    own[3].wait()
    arrive(s1)
    start(s2)
    arrive(w1)
    start(w2)
    arrive(v1)
    start(v2)
    arrive(s2)
    start(s3)
    arrive(w2)
    start(w3)
    arrive(v2)
    start(v3)
    own[0].wait()
    own[1].wait()
    arrive(edges[0:2])
    clear_columns(place, src)
    arrive(s3)

    small = sg.reshape(128, C)[...]
    small_t = small.T
    for n in range(K * K):
        taps[n] = jnp.broadcast_to(small_t[TAPS + n : TAPS + n + 1, :], (8, C))
    conv_bias = jnp.broadcast_to(small_t[CB : CB + 1, :], (8, C))

    def conv_step(b, carry):
        for wb in range(W // 8):
            acc = conv_tile(src, taps, b, wb, False, INNER, {p: conv_bias for p in range(H)})
            for p in range(H):
                mid[b, p, 8 * wb : 8 * wb + 8, :] = acc[p]
        return carry

    lax.fori_loop(0, B, conv_step, 0)
    arrive(edges[2:])
    clear_rows(place, src)

    def conv_rest(b, carry):
        for wb in range(W // 8):
            at = slice(8 * wb, 8 * wb + 8)
            acc = conv_tile(src, taps, b, wb, False, OUTER, {p: mid[b, p, at, :] for p in FRINGE})
            for p in FRINGE:
                mid[b, p, at, :] = acc[p]
        return carry

    lax.fori_loop(0, B, conv_rest, 0)

    arrive(w3)
    arrive(v3)
    gain_wide, shift_wide = widen(small[:, GAIN : GAIN + 1], 4), widen(small[:, SHIFT : SHIFT + 1], 4)
    scale_wide, ob_wide = widen(small[:, SCALE : SCALE + 1], 4), widen(small[:, OB : OB + 1], 1)
    win_t = wg.at[0].reshape(HID, C)[...]
    win = win_t.T
    wo_t = wg.at[1].reshape(HID, C)[...].T
    hi, lo = split(win * gain_wide)
    win2[0:C, :] = hi
    win2[C:, :] = hi
    winlo[...] = lo
    hi, lo = split(win_t * small_t[GAIN : GAIN + 1, :])
    wintop[:, 0:C] = hi
    wintop[:, C:] = lo
    hi, lo = split(wo_t * scale_wide)
    wot2[0:C, :] = hi
    wot2[C:, :] = hi
    wotlo[...] = lo
    pick = [lanes(32, 128, 1) == 4 * lanes(32, 128, 0) + k for k in range(4)]
    shifted = win * shift_wide
    for t in range(4):
        cut, band = slice(128 * t, 128 * t + 128), slice(32 * t, 32 * t + 32)
        terms = [jnp.where(pick[k], small[band, IB + k : IB + k + 1], 0.0) for k in range(4)]
        bias_eff[:, cut] = jnp.sum(shifted[:, cut], axis=0, keepdims=True) + jnp.sum(sum(terms), axis=0, keepdims=True)

    def mix(b, starts):
        spans = [slice(p, p + QUARTER) for p in starts]
        x = jnp.concatenate([mid[b, s].reshape(M // 2, C) for s in spans], axis=0)
        ct = jnp.concatenate([cot[b, s].reshape(M // 2, C) for s in spans], axis=0)
        mean = jnp.mean(x, axis=-1, keepdims=True)
        cen = x - mean
        inv = lax.rsqrt(jnp.mean(cen * cen, axis=-1, keepdims=True) + norm_eps)
        normed = cen * inv
        n_hi, n_lo = split(normed)
        n2 = jnp.concatenate([n_hi, n_lo], axis=1)
        c_hi, c_lo = split(ct)
        c2 = jnp.concatenate([c_hi, c_lo], axis=1)
        nt2 = jnp.concatenate(split(normed.T), axis=0)
        ct2 = jnp.concatenate(split(ct.T), axis=0)
        cotacc[...] += jnp.sum(ct.reshape(M // 8, 8, C), axis=0)
        dn = jnp.zeros((M, C), f32)
        step = 256
        for h in range(0, HID, step):
            cut = slice(h, h + step)
            act = dot(n2, win2[:, cut]) + dot(n_hi, winlo[:, cut]) + bias_eff[:, cut]
            dh = dot(c2, wot2[:, cut]) + dot(c_hi, wotlo[:, cut])
            phi = 0.5 * (1.0 + lax.erf(act * inverse_root_two))
            slope = phi + act * jnp.exp(-0.5 * act * act) * inverse_root_twopi
            hid_hi, hid_lo = split(act * phi)
            da = dh * slope
            inbacc[:, cut] += jnp.sum(da.reshape(M // 8, 8, step), axis=0)
            da_hi, da_lo = split(da)
            both = dot(da_hi, wintop[cut, :])
            dn = dn + both[:, 0:C] + both[:, C:] + dot(da_lo, wintop[cut, 0:C])
            both = dot(nt2, da_hi)
            nacc[:, cut] += both[0:C] + both[C:] + dot(nt2[0:C], da_lo)
            both = dot(ct2, hid_hi)
            macc[:, cut] += both[0:C] + both[C:] + dot(ct2[0:C], hid_lo)
        dc = inv * (
            dn
            - jnp.mean(dn, axis=-1, keepdims=True)
            - normed * jnp.mean(dn * normed, axis=-1, keepdims=True)
        )
        dbacc[...] += jnp.sum(dc.reshape(M // 8, 8, C), axis=0)
        for n, p in enumerate(starts):
            part = dc[n * (M // 2) : (n + 1) * (M // 2)]
            dcv[b, R + p : R + p + QUARTER, LEFT : LEFT + W, :] = part.reshape(QUARTER, W, C)

    def edge_step(b, carry):
        mix(b, (0, H - QUARTER))
        return carry

    def inner_step(b, carry):
        mix(b, (QUARTER, 2 * QUARTER))
        return carry

    lax.fori_loop(0, B, edge_step, 0)
    back = edge_copies(place, dcv, R, LEFT, dcv, dsend, drecv)
    start(back[2:])
    lax.fori_loop(0, B, inner_step, 0)
    start(back[0:2])

    factor = 1.0 / math.sqrt(B * H * W * ROWS * COLS)
    nsum, msum = nacc[...], macc[...]
    inb = jnp.sum(inbacc[...], axis=0, keepdims=True)
    wp[0] = ((nsum * gain_wide + shift_wide * inb) * factor).T.reshape(4, 4, 4, 8, C)
    wp[1] = (msum * (scale_wide * factor)).T.reshape(4, 4, 4, 8, C)
    r0 = [remote(wp.at[1 - core], wcore, 0, place.sibling(), rssend, rsrecv)]
    start(r0)

    def kgrad_step(b, carry):
        for wb in range(W // 8):
            kernel_grad_tile(src, dcv, kacc, b, wb)
        return carry

    lax.fori_loop(0, 1, kgrad_step, 0)
    arrive(r0)
    for a in range(4):
        for b in range(4):
            yy, xx = a * (1 - core) + b * core, b * (1 - core) + a * core
            wa[a, :, b] = wp[core, yy, :, xx] + wcore[yy, :, xx]
    first, second = y * (1 - core) + x * core, x * (1 - core) + y * core
    r1, r2, r3 = [], [], []
    for off in range(1, 4):
        to = place.turn(y=off * (1 - core), x=off * core)[3]
        r1.append(remote(wa.at[lax.rem(first + off, 4)], wr1.at[off - 1], off, to, rssend, rsrecv))
        to = place.turn(y=off * core, x=off * (1 - core))[3]
        r2.append(remote(wb_.at[lax.rem(second + off, 4)], wr2.at[off - 1], 3 + off, to, rssend, rsrecv))
        zz, to = place.turn(z=off)[1::2]
        r3.append(remote(wc.at[zz], wr3.at[off - 1], 6 + off, to, rssend, rsrecv))
    r4 = [remote(wd, wr4, 10, place.sibling(), rssend, rsrecv)]
    start(r1)
    lax.fori_loop(1, 2, kgrad_step, 0)

    gain_g = jnp.sum(win * nsum, axis=1, keepdims=True)
    shift_g = jnp.sum(win * inb, axis=1, keepdims=True)
    scale_g = jnp.sum(wo_t * msum, axis=1, keepdims=True)
    for n in range(K * K):
        rows[n : n + 1, :] = jnp.sum(kacc[n], axis=0, keepdims=True)
    rows[K * K : K * K + 1, :] = jnp.sum(dbacc[...], axis=0, keepdims=True)
    rows[K * K + 1 : K * K + 2, :] = jnp.sum(cotacc[...], axis=0, keepdims=True)
    rows[K * K + 2 :, :] = jnp.zeros((128 - K * K - 2, C), f32)
    grads = rows[...].T
    lane = lanes(C, 128, 1)
    cot_wide = widen(grads[:, K * K + 1 : K * K + 2], 1)
    columns = [(GAIN, gain_g), (SHIFT, shift_g), (OB, scale_wide[:, 0:C] * cot_wide), (SCALE, scale_g + ob_wide * cot_wide)]
    for k in range(4):
        terms = [jnp.where(pick[k], inb[:, 128 * t : 128 * t + 128], 0.0) for t in range(4)]
        columns.append((IB + k, jnp.sum(jnp.concatenate(terms, axis=0), axis=1, keepdims=True)))
    for at, column in columns:
        grads = jnp.where(lane == at, column, grads)
    sp[...] = grads * factor
    q1, q2, q3 = [], [], []
    for off in range(1, 4):
        yy, _, _, to = place.turn(y=off)
        q1.append(remote(sp.at[pl.ds(yy * 32, 32)], sry.at[off - 1], 10 + off, to, rssend, rsrecv))
        zz, to = place.turn(z=off)[1::2]
        q2.append(remote(sb.at[pl.ds(zz * 8, 8)], srz.at[off - 1], 13 + off, to, rssend, rsrecv))
    for off in range(1, 8):
        q3.append(remote(srx.at[0], srx.at[off], 16 + off, place.in_plane(off), rssend, rsrecv))
    start(q1)

    arrive(back[0:2])
    clear_columns(place, dcv)

    def out_step(b, carry):
        for wb in range(W // 8):
            at = slice(8 * wb, 8 * wb + 8)
            acc = conv_tile(dcv, taps, b, wb, True, INNER, {p: cot[b, p, at, :] for p in range(H)})
            for p in range(H):
                fg[b, p, at, :] = acc[p]
        return carry

    def out_rest(b, carry):
        for wb in range(W // 8):
            at = slice(8 * wb, 8 * wb + 8)
            acc = conv_tile(dcv, taps, b, wb, True, OUTER, {p: fg[b, p, at, :] for p in FRINGE})
            for p in FRINGE:
                fg[b, p, at, :] = acc[p]
        return carry

    lax.fori_loop(0, 1, out_step, 0)
    arrive(r1)
    for n in range(4):
        wb_[n] = wa[first, :, n] + wr1[0, :, n] + wr1[1, :, n] + wr1[2, :, n]
    start(r2)
    arrive(q1)
    sb[...] = sp[pl.ds(y * 32, 32)] + sry[0] + sry[1] + sry[2]
    start(q2)
    lax.fori_loop(1, 2, out_step, 0)
    arrive(r2)
    wc[...] = wb_[second] + wr2[0] + wr2[1] + wr2[2]
    start(r3)
    arrive(q2)
    srx[0] = sb[pl.ds(z * 8, 8)] + srz[0] + srz[1] + srz[2]
    start(q3)
    arrive(back[2:])
    clear_rows(place, dcv)
    lax.fori_loop(0, B, out_rest, 0)
    put = pltpu.make_async_copy(fg, fg_out, out_sem.at[0])
    put.start()

    arrive(r3)
    wd[...] = wc[z] + wr3[0] + wr3[1] + wr3[2]
    start(r4)
    arrive(q3)
    total = srx[0]
    for off in range(1, 8):
        total = total + srx[off]
    mine = lanes(8, C, 0) == place.g
    small_out[...] = jnp.sum(jnp.where(mine, total, 0.0), axis=0, keepdims=True)
    arrive(r4)
    kept, got = wd[...], wr4[...]
    weight_out[core] = jnp.where(core == 0, kept[0:4], kept[4:8])
    weight_out[1 - core] = jnp.where(core == 0, got[0:4], got[4:8])

    put.wait()
    for copy in s1 + w1 + v1 + s2 + w2 + v2 + s3 + w3 + v3 + edges + back + r0 + r1 + r2 + r3 + r4 + q1 + q2 + q3:
        copy.wait_send()


def deliver(
    fg_in, small_in, weight_in,
    fg_out, taps_out, cb_out, gain_out, shift_out, win_out, ib_out, wout_out, ob_out, scale_out,
    buf, row, sem,
):
    pieces = [(b, pl.ds(h, H // 2)) for b in range(B) for h in range(0, H, H // 2)]
    small = pltpu.make_async_copy(small_in, row, sem.at[8])
    weights = [pltpu.make_async_copy(weight_in.at[k], ref, sem.at[9 + k]) for k, ref in enumerate((win_out, wout_out))]
    small.start()
    gets = [pltpu.make_async_copy(fg_in.at[at], buf.at[at], sem.at[n]) for n, at in enumerate(pieces)]
    puts = [pltpu.make_async_copy(buf.at[at], fg_out.at[at], sem.at[4 + n]) for n, at in enumerate(pieces)]
    for copy in gets + weights:
        copy.start()
    small.wait()
    for i in range(K):
        for j in range(K):
            taps_out[i, 0, j] = row[0, TAPS + i * K + j]
    for at, ref in ((CB, cb_out), (GAIN, gain_out), (SHIFT, shift_out), (OB, ob_out), (SCALE, scale_out)):
        ref[0] = row[0, at]
    for k in range(4):
        ib_out[k] = row[0, IB + k]
    for get, put in zip(gets, puts):
        get.wait()
        put.start()
    for copy in weights + puts:
        copy.wait()


def per_device(
    features, cotangent, conv_kernel, conv_bias, norm_gain, norm_shift,
    w_in, in_bias, w_out, out_bias, layer_scale,
):
    vmem = lambda *shape: pltpu.VMEM(shape, f32)
    smem = lambda *shape: pltpu.SMEM(shape, f32)
    half = lambda *shape: pltpu.VMEM(shape, bf16)
    dma = lambda n: pltpu.SemaphoreType.DMA((n,))
    out = lambda *shape: jax.ShapeDtypeStruct(shape, f32)
    anywhere = pl.BlockSpec(memory_space=pl.ANY)
    inside = pl.BlockSpec(memory_space=pltpu.VMEM)
    scalar = pl.BlockSpec(memory_space=pltpu.SMEM)
    tile = (B, H, W, C)
    fg, small, weights = pl.pallas_call(
        kernel,
        out_shape=(out(*tile), out(1, C), out(2, 4, C)),
        in_specs=[anywhere] * 11,
        out_specs=(anywhere, inside, inside),
        scratch_shapes=[
            smem(K, 1, K), smem(1), smem(1), smem(1), smem(1), smem(1), smem(4), vmem(1, C),
            vmem(B, HE, WE, C), vmem(*tile), vmem(B, HE, WE, C), vmem(*tile), vmem(*tile),
            vmem(4, 4, 4, 2, 1, C), vmem(2, 4, 4, 4, 2, 4, C), vmem(K * K, 8, C),
            half(2 * C, HID), half(C, HID), half(HID, 2 * C), half(2 * C, HID), half(C, HID), vmem(1, HID),
            vmem(C, HID), vmem(C, HID), vmem(8, HID), vmem(K * K, 8, C), vmem(8, C), vmem(8, C),
            vmem(2, 4, 4, 4, 8, C), vmem(4, 4, 4, 8, C), vmem(4, 4, 4, 8, C), vmem(3, 4, 4, 8, C),
            vmem(4, 4, 8, C), vmem(3, 4, 8, C), vmem(4, 8, C), vmem(3, 8, C), vmem(8, C), vmem(8, C),
            vmem(128, C), vmem(128, C), vmem(3, 32, C), vmem(32, C), vmem(3, 8, C), vmem(8, 8, C),
            dma(11), dma(1), dma(8), dma(8), dma(8), dma(8), dma(39), dma(39), dma(24), dma(24),
        ],
        compiler_params=pltpu.CompilerParams(
            collective_id=0, has_side_effects=True, vmem_limit_bytes=56 * 2**20
        ),
    )(
        features, cotangent, conv_kernel.transpose(0, 2, 1), conv_bias, norm_gain, norm_shift,
        out_bias, layer_scale, in_bias, w_in.T, w_out,
    )
    fg, taps_g, cb_g, gain_g, shift_g, win_g, ib_g, wout_g, ob_g, scale_g = pl.pallas_call(
        deliver,
        out_shape=(
            out(*tile), out(K, 1, K), out(1), out(1), out(1), out(4, C), out(4), out(4, C), out(1), out(1),
        ),
        in_specs=[anywhere] * 3,
        out_specs=(anywhere, scalar, scalar, scalar, scalar, inside, scalar, inside, scalar, scalar),
        scratch_shapes=[vmem(*tile), smem(1, C), dma(11)],
    )(fg, small, weights)
    return fg, taps_g.transpose(0, 2, 1), cb_g, gain_g, shift_g, win_g.T, ib_g, wout_g, ob_g, scale_g


def solution(mesh):
    both = ("row", "col")
    tile = P(None, "row", "col", None)
    taps, vector = P(None, None, both), P(both)
    return jax.shard_map(
        per_device,
        mesh=mesh,
        in_specs=(tile, tile, taps, vector, vector, vector, P(None, both), vector, P(both, None), vector, vector),
        out_specs=(tile, taps, vector, vector, vector, P(None, both), vector, P(both, None), vector, vector),
        check_vma=False,
    )
```

time: 73 us -> 63.1 us (0.86)
  local copies, waits for them, and re-layouts: 6.85 us -> 0 us
  Pallas kernels: 61.3 us -> 58.8 us
    unnamed x13 -> x0, local copies, waits for them, and re-layouts: 3.73 us -> none
    pallas_call x1 -> x2, Pallas kernels: 61.3 us -> 58.8 us  [the longest x1 56.2 us: per_device(): pl.pallas_call(kernel, out_shape=(out(*tile), out(1, C), out(2, 4, C)), i...]
    slice x3 -> x0, local copies, waits for them, and re-layouts: 1.2 us -> none  [the longest x1 0.6 us: per_device(): row[SCALE:SCALE + 1]]
    reshape x2 -> x0, local copies, waits for them, and re-layouts: 0.74 us -> none  [the longest x1 0.66 us: per_device(): row[0:K * K].reshape(K, K, 1)]
where the time goes in v2:
time: 63.1 us; the launch traced here: 62.9 us
  Pallas kernels  58.8 us (93%)
  between operations  4.06 us (6%)
    pallas_call x1, Pallas kernels, per_device(): pl.pallas_call(kernel, out_shape=(out(*tile), out(1, C), out(2, 4, C)), i...  56.2 us
    pallas_call x1, Pallas kernels, per_device(): pl.pallas_call(deliver, out_shape=(out(*tile), out(K, 1, K), out(1), out(...  2.63 us

profile of v2, /device:TPU:1, one launch (start us, length us, event | category | flops | bytes accessed | tf_op | source)
XLA Modules:
  0.0 62.9 jit_solution(1588094448746226312)
XLA Ops:
  3.9 56.2 %shard_map.186 = (f32[2,16,64,128]{3,2,1,0:T(8,128)}, f32[1,128]{1,0:T(1,128)}, f32[2,4,128]{2,1,0:T(4,128)}) custom-call(f32[2,16,64,128]{3,2,1,0:T(8,128)} %feat.1, f32[2,16,64,128]{3,2,1,0:T(8,128)} %cot_hbm.1, f32[7,1,7]{2,1,0:T(1,128)} %bitcast.4, f32[1]{0:T(128)S(6)} %copy.21.cb_in, f32[1]{0:T(128)S(6)} %copy.22.gain_in, f32[1]{0:T(128)S(6)} %copy.23.shift_in, ...), custom_call_target="tpu_custom_call" | custom-call | tf_op jit(solution)/shard_map/pallas_call | solution.py:548
  60.1 2.6 %shard_map.187 = (f32[2,16,64,128]{3,2,1,0:T(8,128)}, f32[7,1,7]{2,1,0:T(1,128)}, f32[1]{0:T(128)}, f32[1]{0:T(128)}, f32[1]{0:T(128)}, /*index=5*/f32[4,128]{1,...) custom-call(f32[2,16,64,128]{3,2,1,0:T(8,128)} %get-tuple-element.23.fg_in, ...), custom_call_target="tpu_custom_call" | custom-call | tf_op jit(solution)/shard_map/pallas_call | solution.py:571

commit v3 on v2

--- a/solution.py
+++ b/solution.py
@@ -22,6 +22,7 @@
 HE = H + 2 * R
 ROWS, COLS = 8, 16
 QUARTER = H // 4
+BLOCKS = B * W // 8
 M = 2 * QUARTER * W
 TAPS, CB, GAIN, SHIFT, OB, SCALE, IB = 0, 49, 50, 51, 52, 53, 54
 
@@ -56,7 +57,7 @@
 
     def in_plane(self, off):
         other = lax.rem(self.g + off, 8)
-        return self.at(self.y, self.z, other // 2, lax.rem(other, 2))
+        return other, self.at(self.y, self.z, other // 2, lax.rem(other, 2))
 
     def in_column(self, off):
         other = lax.rem(self.z * 2 + self.core + off, 8)
@@ -134,7 +135,7 @@
     for j in range(K):
         tap = [taps[(K - 1 - i) * K + K - 1 - j] if flip else taps[i * K + j] for i in range(K)]
         for e in rows:
-            x = ext[b, e, LEFT - R + 8 * wb + j : LEFT - R + 8 * wb + j + 8, :]
+            x = ext[b, e, pl.ds(8 * wb + LEFT - R + j, 8), :]
             for i in range(K):
                 p = e - i
                 if 0 <= p < H:
@@ -148,11 +149,11 @@
 
 
 def kernel_grad_tile(ext, dcv, kacc, b, wb):
-    grads = [dcv[b, R + p, LEFT + 8 * wb : LEFT + 8 * wb + 8, :] for p in range(H)]
+    grads = [dcv[b, R + p, pl.ds(pl.multiple_of(8 * wb + LEFT, 8), 8), :] for p in range(H)]
     for j in range(K):
         acc = [kacc[i * K + j] for i in range(K)]
         for e in range(HE):
-            x = ext[b, e, LEFT - R + 8 * wb + j : LEFT - R + 8 * wb + j + 8, :]
+            x = ext[b, e, pl.ds(8 * wb + LEFT - R + j, 8), :]
             for i in range(K):
                 p = e - i
                 if 0 <= p < H:
@@ -173,7 +174,7 @@
     src, cot, dcv, mid, fg, sg, wg, taps,
     win2, winlo, wintop, wot2, wotlo, bias_eff,
     nacc, macc, inbacc, kacc, cotacc, dbacc,
-    wp, wcore, wa, wr1, wb_, wr2, wc, wr3, wd, wr4, rows, sp, sry, sb, srz, srx,
+    wp, wcore, wa, wr1, wb_, wr2, wc, wr3, wd, wr4, rows, sp, srx, sb, sry, sc, srz,
     local, out_sem, fsend, frecv, dsend, drecv, agsend, agrecv, rssend, rsrecv,
 ):
     place = Place()
@@ -192,7 +193,7 @@
 
     barrier = pltpu.get_barrier_semaphore()
     partners = [place.neighbour(dr, dc) for dr, dc in STEPS]
-    partners += [place.in_plane(off) for off in range(1, 8)]
+    partners += [place.in_plane(off)[1] for off in range(1, 8)]
     partners += [place.in_column(off) for off in range(1, 8)]
     partners += [place.turn(y=off)[3] for off in range(1, 4)]
     for partner in partners:
@@ -236,10 +237,10 @@
     s1 = [remote(srow, sg.at[cell], n, p, agsend, agrecv) for n, p in enumerate(group)]
     w1 = [remote(win_in, wg.at[(0, *cell)], 7 + n, p, agsend, agrecv) for n, p in enumerate(group)]
     v1 = [remote(wout_in, wg.at[(1, *cell)], 14 + n, p, agsend, agrecv) for n, p in enumerate(group)]
-    s2 = [same(sg.at[y, :, x], 21 + n, p) for n, p in enumerate(xs)]
+    s2 = [same(sg.at[y, :, x], 21 + n, p) for n, p in enumerate(ys)]
     w2 = [same(wg.at[0, y, :, x], 24 + n, p) for n, p in enumerate(xs)]
     v2 = [same(wg.at[1, y, :, x], 27 + n, p) for n, p in enumerate(ys)]
-    s3 = [same(sg.at[y], 30 + n, p) for n, p in enumerate(ys)]
+    s3 = [same(sg.at[:, :, x], 30 + n, p) for n, p in enumerate(xs)]
     w3 = [same(wg.at[0, y], 33 + n, p) for n, p in enumerate(ys)]
     v3 = [same(wg.at[1, :, :, x], 36 + n, p) for n, p in enumerate(xs)]
     edges = edge_copies(place, feat, 0, 0, src, fsend, frecv)
@@ -252,10 +253,14 @@
         for copy in copies:
             copy.wait_recv()
 
+    def leave(copies):
+        for copy in copies:
+            copy.wait_send()
+
     start(s1)
     start(w1)
     start(v1)
-    start(edges)
+    start(edges[0:2])
     own[2].wait()
     own[3].wait()
     arrive(s1)
@@ -264,6 +269,7 @@
     start(w2)
     arrive(v1)
     start(v2)
+    start(edges[2:])
     arrive(s2)
     start(s3)
     arrive(w2)
@@ -282,26 +288,24 @@
         taps[n] = jnp.broadcast_to(small_t[TAPS + n : TAPS + n + 1, :], (8, C))
     conv_bias = jnp.broadcast_to(small_t[CB : CB + 1, :], (8, C))
 
-    def conv_step(b, carry):
-        for wb in range(W // 8):
-            acc = conv_tile(src, taps, b, wb, False, INNER, {p: conv_bias for p in range(H)})
-            for p in range(H):
-                mid[b, p, 8 * wb : 8 * wb + 8, :] = acc[p]
+    def column_block(n):
+        return n // 8, lax.rem(n, 8), pl.ds(pl.multiple_of(lax.rem(n, 8) * 8, 8), 8)
+
+    def conv_step(n, carry):
+        b, wb, at = column_block(n)
+        acc = conv_tile(src, taps, b, wb, False, INNER, {p: conv_bias for p in range(H)})
+        for p in range(H):
+            mid[b, p, at, :] = acc[p]
         return carry
 
-    lax.fori_loop(0, B, conv_step, 0)
-    arrive(edges[2:])
-    clear_rows(place, src)
-
-    def conv_rest(b, carry):
-        for wb in range(W // 8):
-            at = slice(8 * wb, 8 * wb + 8)
-            acc = conv_tile(src, taps, b, wb, False, OUTER, {p: mid[b, p, at, :] for p in FRINGE})
-            for p in FRINGE:
-                mid[b, p, at, :] = acc[p]
+    lax.fori_loop(0, BLOCKS, conv_step, 0)
+
+    def conv_rest(n, carry):
+        b, wb, at = column_block(n)
+        acc = conv_tile(src, taps, b, wb, False, OUTER, {p: mid[b, p, at, :] for p in FRINGE})
+        for p in FRINGE:
+            mid[b, p, at, :] = acc[p]
         return carry
-
-    lax.fori_loop(0, B, conv_rest, 0)
 
     arrive(w3)
     arrive(v3)
@@ -329,7 +333,7 @@
         bias_eff[:, cut] = jnp.sum(shifted[:, cut], axis=0, keepdims=True) + jnp.sum(sum(terms), axis=0, keepdims=True)
 
     def mix(b, starts):
-        spans = [slice(p, p + QUARTER) for p in starts]
+        spans = [pl.ds(p, QUARTER) for p in starts]
         x = jnp.concatenate([mid[b, s].reshape(M // 2, C) for s in spans], axis=0)
         ct = jnp.concatenate([cot[b, s].reshape(M // 2, C) for s in spans], axis=0)
         mean = jnp.mean(x, axis=-1, keepdims=True)
@@ -369,20 +373,27 @@
         dbacc[...] += jnp.sum(dc.reshape(M // 8, 8, C), axis=0)
         for n, p in enumerate(starts):
             part = dc[n * (M // 2) : (n + 1) * (M // 2)]
-            dcv[b, R + p : R + p + QUARTER, LEFT : LEFT + W, :] = part.reshape(QUARTER, W, C)
-
-    def edge_step(b, carry):
-        mix(b, (0, H - QUARTER))
+            dcv[b, pl.ds(R + p, QUARTER), LEFT : LEFT + W, :] = part.reshape(QUARTER, W, C)
+
+    back = edge_copies(place, dcv, R, LEFT, dcv, dsend, drecv)
+
+    def mix_step(n, carry):
+        outer = lax.rem((n + 1) // 2, 2)
+
+        @pl.when(n == 1)
+        def _():
+            arrive(edges[2:])
+            clear_rows(place, src)
+            lax.fori_loop(0, BLOCKS, conv_rest, 0)
+
+        @pl.when(n == 3)
+        def _():
+            start(back[2:])
+
+        mix(n // 2, (QUARTER * (1 - outer), QUARTER * (2 + outer)))
         return carry
 
-    def inner_step(b, carry):
-        mix(b, (QUARTER, 2 * QUARTER))
-        return carry
-
-    lax.fori_loop(0, B, edge_step, 0)
-    back = edge_copies(place, dcv, R, LEFT, dcv, dsend, drecv)
-    start(back[2:])
-    lax.fori_loop(0, B, inner_step, 0)
+    lax.fori_loop(0, 4, mix_step, 0)
     start(back[0:2])
 
     factor = 1.0 / math.sqrt(B * H * W * ROWS * COLS)
@@ -393,12 +404,11 @@
     r0 = [remote(wp.at[1 - core], wcore, 0, place.sibling(), rssend, rsrecv)]
     start(r0)
 
-    def kgrad_step(b, carry):
-        for wb in range(W // 8):
-            kernel_grad_tile(src, dcv, kacc, b, wb)
+    def kgrad_step(n, carry):
+        kernel_grad_tile(src, dcv, kacc, n // 8, lax.rem(n, 8))
         return carry
 
-    lax.fori_loop(0, 1, kgrad_step, 0)
+    lax.fori_loop(0, BLOCKS // 2, kgrad_step, 0)
     arrive(r0)
     for a in range(4):
         for b in range(4):
@@ -415,7 +425,7 @@
         r3.append(remote(wc.at[zz], wr3.at[off - 1], 6 + off, to, rssend, rsrecv))
     r4 = [remote(wd, wr4, 10, place.sibling(), rssend, rsrecv)]
     start(r1)
-    lax.fori_loop(1, 2, kgrad_step, 0)
+    lax.fori_loop(BLOCKS // 2, BLOCKS, kgrad_step, 0)
 
     gain_g = jnp.sum(win * nsum, axis=1, keepdims=True)
     shift_g = jnp.sum(win * inb, axis=1, keepdims=True)
@@ -434,74 +444,74 @@
         columns.append((IB + k, jnp.sum(jnp.concatenate(terms, axis=0), axis=1, keepdims=True)))
     for at, column in columns:
         grads = jnp.where(lane == at, column, grads)
-    sp[...] = grads * factor
+    sp.reshape(128, C)[...] = grads * factor
     q1, q2, q3 = [], [], []
+    for off in range(1, 8):
+        g, to = place.in_plane(off)
+        q1.append(remote(sp.at[:, :, g // 2, lax.rem(g, 2)], srx.at[off - 1], 10 + off, to, rssend, rsrecv))
     for off in range(1, 4):
         yy, _, _, to = place.turn(y=off)
-        q1.append(remote(sp.at[pl.ds(yy * 32, 32)], sry.at[off - 1], 10 + off, to, rssend, rsrecv))
+        q2.append(remote(sb.at[yy], sry.at[off - 1], 17 + off, to, rssend, rsrecv))
         zz, to = place.turn(z=off)[1::2]
-        q2.append(remote(sb.at[pl.ds(zz * 8, 8)], srz.at[off - 1], 13 + off, to, rssend, rsrecv))
-    for off in range(1, 8):
-        q3.append(remote(srx.at[0], srx.at[off], 16 + off, place.in_plane(off), rssend, rsrecv))
+        q3.append(remote(sc.at[zz], srz.at[off - 1], 20 + off, to, rssend, rsrecv))
     start(q1)
 
     arrive(back[0:2])
     clear_columns(place, dcv)
 
-    def out_step(b, carry):
-        for wb in range(W // 8):
-            at = slice(8 * wb, 8 * wb + 8)
-            acc = conv_tile(dcv, taps, b, wb, True, INNER, {p: cot[b, p, at, :] for p in range(H)})
-            for p in range(H):
-                fg[b, p, at, :] = acc[p]
+    def out_step(n, carry):
+        b, wb, at = column_block(n)
+        acc = conv_tile(dcv, taps, b, wb, True, INNER, {p: cot[b, p, at, :] for p in range(H)})
+        for p in range(H):
+            fg[b, p, at, :] = acc[p]
         return carry
 
-    def out_rest(b, carry):
-        for wb in range(W // 8):
-            at = slice(8 * wb, 8 * wb + 8)
-            acc = conv_tile(dcv, taps, b, wb, True, OUTER, {p: fg[b, p, at, :] for p in FRINGE})
-            for p in FRINGE:
-                fg[b, p, at, :] = acc[p]
+    def out_rest(n, carry):
+        b, wb, at = column_block(n)
+        acc = conv_tile(dcv, taps, b, wb, True, OUTER, {p: fg[b, p, at, :] for p in FRINGE})
+        for p in FRINGE:
+            fg[b, p, at, :] = acc[p]
         return carry
 
-    lax.fori_loop(0, 1, out_step, 0)
+    lax.fori_loop(0, 6, out_step, 0)
     arrive(r1)
     for n in range(4):
         wb_[n] = wa[first, :, n] + wr1[0, :, n] + wr1[1, :, n] + wr1[2, :, n]
     start(r2)
+    lax.fori_loop(6, 9, out_step, 0)
     arrive(q1)
-    sb[...] = sp[pl.ds(y * 32, 32)] + sry[0] + sry[1] + sry[2]
+    total = sp[:, :, x, core]
+    for n in range(7):
+        total = total + srx[n]
+    sb[...] = total
     start(q2)
-    lax.fori_loop(1, 2, out_step, 0)
+    lax.fori_loop(9, 13, out_step, 0)
     arrive(r2)
     wc[...] = wb_[second] + wr2[0] + wr2[1] + wr2[2]
     start(r3)
     arrive(q2)
-    srx[0] = sb[pl.ds(z * 8, 8)] + srz[0] + srz[1] + srz[2]
+    sc[...] = sb[y] + sry[0] + sry[1] + sry[2]
     start(q3)
+    lax.fori_loop(13, BLOCKS, out_step, 0)
     arrive(back[2:])
     clear_rows(place, dcv)
-    lax.fori_loop(0, B, out_rest, 0)
+    lax.fori_loop(0, BLOCKS, out_rest, 0)
     put = pltpu.make_async_copy(fg, fg_out, out_sem.at[0])
     put.start()
 
+    leave(s1 + w1 + v1 + s2 + w2 + v2 + s3 + w3 + v3 + edges + back + r0 + r1 + r2 + q1 + q2)
     arrive(r3)
     wd[...] = wc[z] + wr3[0] + wr3[1] + wr3[2]
     start(r4)
     arrive(q3)
-    total = srx[0]
-    for off in range(1, 8):
-        total = total + srx[off]
-    mine = lanes(8, C, 0) == place.g
-    small_out[...] = jnp.sum(jnp.where(mine, total, 0.0), axis=0, keepdims=True)
+    small_out[...] = sc[z] + srz[0] + srz[1] + srz[2]
     arrive(r4)
     kept, got = wd[...], wr4[...]
     weight_out[core] = jnp.where(core == 0, kept[0:4], kept[4:8])
     weight_out[1 - core] = jnp.where(core == 0, got[0:4], got[4:8])
 
     put.wait()
-    for copy in s1 + w1 + v1 + s2 + w2 + v2 + s3 + w3 + v3 + edges + back + r0 + r1 + r2 + r3 + r4 + q1 + q2 + q3:
-        copy.wait_send()
+    leave(r3 + r4 + q3)
 
 
 def deliver(
@@ -558,7 +568,7 @@
             vmem(C, HID), vmem(C, HID), vmem(8, HID), vmem(K * K, 8, C), vmem(8, C), vmem(8, C),
             vmem(2, 4, 4, 4, 8, C), vmem(4, 4, 4, 8, C), vmem(4, 4, 4, 8, C), vmem(3, 4, 4, 8, C),
             vmem(4, 4, 8, C), vmem(3, 4, 8, C), vmem(4, 8, C), vmem(3, 8, C), vmem(8, C), vmem(8, C),
-            vmem(128, C), vmem(128, C), vmem(3, 32, C), vmem(32, C), vmem(3, 8, C), vmem(8, 8, C),
+            vmem(128, C), vmem(4, 4, 4, 2, 1, C), vmem(7, 4, 4, 1, C), vmem(4, 4, 1, C), vmem(3, 4, 1, C), vmem(4, 1, C), vmem(3, 1, C),
             dma(11), dma(1), dma(8), dma(8), dma(8), dma(8), dma(39), dma(39), dma(24), dma(24),
         ],
         compiler_params=pltpu.CompilerParams(

time: 63.1 us -> 58.8 us (0.932)
  Pallas kernels: 58.8 us -> 54.7 us
    pallas_call x1, Pallas kernels: 56.2 us -> 52.1 us  [per_device(): pl.pallas_call(kernel, out_shape=(out(*tile), out(1, C), out(2, 4, C)), i...]
where the time goes in v3:
time: 58.8 us; the launch traced here: 58.6 us
  Pallas kernels  54.7 us (93%)
  between operations  3.88 us (7%)
    pallas_call x1, Pallas kernels, per_device(): pl.pallas_call(kernel, out_shape=(out(*tile), out(1, C), out(2, 4, C)), i...  52.1 us
    pallas_call x1, Pallas kernels, per_device(): pl.pallas_call(deliver, out_shape=(out(*tile), out(K, 1, K), out(1), out(...  2.63 us

profile of v3, /device:TPU:1, one launch (start us, length us, event | category | flops | bytes accessed | tf_op | source)
XLA Modules:
  0.0 58.6 jit_solution(15802903239471346880)
XLA Ops:
  3.9 52.1 %shard_map.186 = (f32[2,16,64,128]{3,2,1,0:T(8,128)}, f32[1,128]{1,0:T(1,128)}, f32[2,4,128]{2,1,0:T(4,128)}) custom-call(f32[2,16,64,128]{3,2,1,0:T(8,128)} %feat.1, f32[2,16,64,128]{3,2,1,0:T(8,128)} %cot_hbm.1, f32[7,1,7]{2,1,0:T(1,128)} %bitcast.4, f32[1]{0:T(128)S(6)} %copy.21.cb_in, f32[1]{0:T(128)S(6)} %copy.22.gain_in, f32[1]{0:T(128)S(6)} %copy.23.shift_in, ...), custom_call_target="tpu_custom_call" | custom-call | tf_op jit(solution)/shard_map/pallas_call | solution.py:558
  56.0 2.6 %shard_map.187 = (f32[2,16,64,128]{3,2,1,0:T(8,128)}, f32[7,1,7]{2,1,0:T(1,128)}, f32[1]{0:T(128)}, f32[1]{0:T(128)}, f32[1]{0:T(128)}, /*index=5*/f32[4,128]{1,...) custom-call(f32[2,16,64,128]{3,2,1,0:T(8,128)} %get-tuple-element.23.fg_in, ...), custom_call_target="tpu_custom_call" | custom-call | tf_op jit(solution)/shard_map/pallas_call | solution.py:581

commit v4 on v3

--- a/solution.py
+++ b/solution.py
@@ -23,6 +23,7 @@
 ROWS, COLS = 8, 16
 QUARTER = H // 4
 BLOCKS = B * W // 8
+CUT = BLOCKS // 2 + 1
 M = 2 * QUARTER * W
 TAPS, CB, GAIN, SHIFT, OB, SCALE, IB = 0, 49, 50, 51, 52, 53, 54
 
@@ -61,7 +62,11 @@
 
     def in_column(self, off):
         other = lax.rem(self.z * 2 + self.core + off, 8)
-        return self.at(self.y, other // 2, self.x, lax.rem(other, 2))
+        return other // 2, self.at(self.y, other // 2, self.x, lax.rem(other, 2))
+
+    def in_wall(self, off):
+        y, z = lax.rem(self.y + off // 4, 4), lax.rem(self.z + off % 4, 4)
+        return y, z, self.at(y, z, self.x, self.core)
 
     def sibling(self):
         return self.at(self.y, self.z, self.x, 1 - self.core)
@@ -89,20 +94,15 @@
     return pl.ds(LEFT + W, LEFT) if step < 0 else pl.ds(0, LEFT)
 
 
-def edge_copies(place, src, row0, col0, ext, send, recv):
-    copies = []
-    for n, (dr, dc) in enumerate(STEPS):
-        copies.append(
-            pltpu.make_async_remote_copy(
-                src_ref=src.at[:, rows_of(dr, row0, True), cols_of(dc, col0, True), :],
-                dst_ref=ext.at[:, rows_of(dr, R, False), cols_of(dc, LEFT, False), :],
-                send_sem=send.at[n],
-                recv_sem=recv.at[n],
-                device_id=place.neighbour(dr, dc),
-                device_id_type=MESH,
-            )
+def edge_ends(place, src, row0, col0, ext):
+    return [
+        (
+            src.at[:, rows_of(dr, row0, True), cols_of(dc, col0, True), :],
+            ext.at[:, rows_of(dr, R, False), cols_of(dc, LEFT, False), :],
+            place.neighbour(dr, dc),
         )
-    return copies
+        for dr, dc in STEPS
+    ]
 
 
 def clear_columns(place, ext):
@@ -174,8 +174,8 @@
     src, cot, dcv, mid, fg, sg, wg, taps,
     win2, winlo, wintop, wot2, wotlo, bias_eff,
     nacc, macc, inbacc, kacc, cotacc, dbacc,
-    wp, wcore, wa, wr1, wb_, wr2, wc, wr3, wd, wr4, rows, sp, srx, sb, sry, sc, srz,
-    local, out_sem, fsend, frecv, dsend, drecv, agsend, agrecv, rssend, rsrecv,
+    wp, wcore, wa, wr1, wb_, wr2, wc, wr3, rows, sp, srx, sb, sry,
+    local, out_sem, sent, arrived,
 ):
     place = Place()
     y, z, x, core = place.y, place.z, place.x, place.core
@@ -194,8 +194,8 @@
     barrier = pltpu.get_barrier_semaphore()
     partners = [place.neighbour(dr, dc) for dr, dc in STEPS]
     partners += [place.in_plane(off)[1] for off in range(1, 8)]
-    partners += [place.in_column(off) for off in range(1, 8)]
-    partners += [place.turn(y=off)[3] for off in range(1, 4)]
+    partners += [place.in_column(off)[1] for off in range(1, 8)]
+    partners += [place.in_wall(off)[2] for off in range(1, 16)]
     for partner in partners:
         pl.semaphore_signal(barrier, inc=1, device_id=partner, device_id_type=MESH)
 
@@ -221,66 +221,72 @@
 
     pl.semaphore_wait(barrier, len(partners))
 
-    def remote(s, d, sem, partner, send, recv):
-        return pltpu.make_async_remote_copy(
-            src_ref=s, dst_ref=d, send_sem=send.at[sem], recv_sem=recv.at[sem],
-            device_id=partner, device_id_type=MESH,
-        )
-
-    def same(ref, sem, partner):
-        return remote(ref, ref, sem, partner, agsend, agrecv)
+    stages = []
+
+    class Stage:
+        def __init__(self, amount, copies):
+            self.n = len(stages)
+            stages.append(self)
+            self.amount = amount
+            self.copies = [self.copy(*ends) for ends in copies]
+
+        def copy(self, a, b, partner):
+            return pltpu.make_async_remote_copy(
+                src_ref=a, dst_ref=b, send_sem=sent.at[self.n], recv_sem=arrived.at[self.n],
+                device_id=partner, device_id_type=MESH,
+            )
+
+        def start(self):
+            for copy in self.copies:
+                copy.start()
+
+        def arrive(self):
+            self.copy(self.amount, self.amount, place.sibling()).wait_recv()
+
+        def leave(self):
+            self.copy(self.amount, self.amount, place.sibling()).wait_send()
 
     cell = (y, z, x, core)
-    group = [place.in_column(off) for off in range(1, 8)]
+    plane = [place.in_plane(off)[1] for off in range(1, 8)]
+    column = [place.in_column(off)[1] for off in range(1, 8)]
+    wall = [place.in_wall(off)[2] for off in range(1, 16)]
     xs = [place.turn(x=off)[3] for off in range(1, 4)]
     ys = [place.turn(y=off)[3] for off in range(1, 4)]
-    s1 = [remote(srow, sg.at[cell], n, p, agsend, agrecv) for n, p in enumerate(group)]
-    w1 = [remote(win_in, wg.at[(0, *cell)], 7 + n, p, agsend, agrecv) for n, p in enumerate(group)]
-    v1 = [remote(wout_in, wg.at[(1, *cell)], 14 + n, p, agsend, agrecv) for n, p in enumerate(group)]
-    s2 = [same(sg.at[y, :, x], 21 + n, p) for n, p in enumerate(ys)]
-    w2 = [same(wg.at[0, y, :, x], 24 + n, p) for n, p in enumerate(xs)]
-    v2 = [same(wg.at[1, y, :, x], 27 + n, p) for n, p in enumerate(ys)]
-    s3 = [same(sg.at[:, :, x], 30 + n, p) for n, p in enumerate(xs)]
-    w3 = [same(wg.at[0, y], 33 + n, p) for n, p in enumerate(ys)]
-    v3 = [same(wg.at[1, :, :, x], 36 + n, p) for n, p in enumerate(xs)]
-    edges = edge_copies(place, feat, 0, 0, src, fsend, frecv)
-
-    def start(copies):
-        for copy in copies:
-            copy.start()
-
-    def arrive(copies):
-        for copy in copies:
-            copy.wait_recv()
-
-    def leave(copies):
-        for copy in copies:
-            copy.wait_send()
-
-    start(s1)
-    start(w1)
-    start(v1)
-    start(edges[0:2])
+    cells = wg.at[0].reshape(128, 4, C)
+    s1 = Stage(srx.at[:, 0, 0], [(srow, sg.at[cell], p) for p in plane])
+    w1 = Stage(cells.at[pl.ds(0, 7)], [(win_in, wg.at[(0, *cell)], p) for p in column])
+    v1 = Stage(cells.at[pl.ds(0, 7)], [(wout_in, wg.at[(1, *cell)], p) for p in column])
+    s2 = Stage(sg.reshape(128, 1, C).at[pl.ds(0, 120)], [(sg.at[y, z], sg.at[y, z], p) for p in wall])
+    w2 = Stage(cells.at[pl.ds(0, 24)], [(wg.at[0, y, :, x], wg.at[0, y, :, x], p) for p in xs])
+    v2 = Stage(cells.at[pl.ds(0, 24)], [(wg.at[1, y, :, x], wg.at[1, y, :, x], p) for p in ys])
+    w3 = Stage(cells.at[pl.ds(0, 96)], [(wg.at[0, y], wg.at[0, y], p) for p in ys])
+    v3 = Stage(cells.at[pl.ds(0, 96)], [(wg.at[1, :, :, x], wg.at[1, :, :, x], p) for p in xs])
+    edges = edge_ends(place, feat, 0, 0, src)
+    side = Stage(src.at[:, pl.ds(0, H), pl.ds(0, 2 * LEFT), :], edges[0:2])
+    ends = Stage(src.at[:, pl.ds(0, 2 * R), :, :], edges[2:])
+
+    s1.start()
+    w1.start()
+    v1.start()
+    side.start()
     own[2].wait()
     own[3].wait()
-    arrive(s1)
-    start(s2)
-    arrive(w1)
-    start(w2)
-    arrive(v1)
-    start(v2)
-    start(edges[2:])
-    arrive(s2)
-    start(s3)
-    arrive(w2)
-    start(w3)
-    arrive(v2)
-    start(v3)
+    s1.arrive()
+    s2.start()
+    w1.arrive()
+    w2.start()
+    v1.arrive()
+    v2.start()
+    ends.start()
+    w2.arrive()
+    w3.start()
+    v2.arrive()
+    v3.start()
     own[0].wait()
     own[1].wait()
-    arrive(edges[0:2])
+    side.arrive()
     clear_columns(place, src)
-    arrive(s3)
+    s2.arrive()
 
     small = sg.reshape(128, C)[...]
     small_t = small.T
@@ -307,8 +313,8 @@
             mid[b, p, at, :] = acc[p]
         return carry
 
-    arrive(w3)
-    arrive(v3)
+    w3.arrive()
+    v3.arrive()
     gain_wide, shift_wide = widen(small[:, GAIN : GAIN + 1], 4), widen(small[:, SHIFT : SHIFT + 1], 4)
     scale_wide, ob_wide = widen(small[:, SCALE : SCALE + 1], 4), widen(small[:, OB : OB + 1], 1)
     win_t = wg.at[0].reshape(HID, C)[...]
@@ -375,57 +381,56 @@
             part = dc[n * (M // 2) : (n + 1) * (M // 2)]
             dcv[b, pl.ds(R + p, QUARTER), LEFT : LEFT + W, :] = part.reshape(QUARTER, W, C)
 
-    back = edge_copies(place, dcv, R, LEFT, dcv, dsend, drecv)
+    back = edge_ends(place, dcv, R, LEFT, dcv)
+    back_side = Stage(src.at[:, pl.ds(0, H), pl.ds(0, 2 * LEFT), :], back[0:2])
+    back_ends = Stage(src.at[:, pl.ds(0, 2 * R), :, :], back[2:])
 
     def mix_step(n, carry):
         outer = lax.rem((n + 1) // 2, 2)
 
         @pl.when(n == 1)
         def _():
-            arrive(edges[2:])
+            ends.arrive()
             clear_rows(place, src)
             lax.fori_loop(0, BLOCKS, conv_rest, 0)
 
         @pl.when(n == 3)
         def _():
-            start(back[2:])
+            back_ends.start()
 
         mix(n // 2, (QUARTER * (1 - outer), QUARTER * (2 + outer)))
         return carry
 
     lax.fori_loop(0, 4, mix_step, 0)
-    start(back[0:2])
+    back_side.start()
 
     factor = 1.0 / math.sqrt(B * H * W * ROWS * COLS)
     nsum, msum = nacc[...], macc[...]
     inb = jnp.sum(inbacc[...], axis=0, keepdims=True)
     wp[0] = ((nsum * gain_wide + shift_wide * inb) * factor).T.reshape(4, 4, 4, 8, C)
     wp[1] = (msum * (scale_wide * factor)).T.reshape(4, 4, 4, 8, C)
-    r0 = [remote(wp.at[1 - core], wcore, 0, place.sibling(), rssend, rsrecv)]
-    start(r0)
+    r0 = Stage(wcore, [(wp.at[1 - core], wcore, place.sibling())])
+    r0.start()
 
     def kgrad_step(n, carry):
         kernel_grad_tile(src, dcv, kacc, n // 8, lax.rem(n, 8))
         return carry
 
-    lax.fori_loop(0, BLOCKS // 2, kgrad_step, 0)
-    arrive(r0)
+    lax.fori_loop(0, CUT, kgrad_step, 0)
+    r0.arrive()
     for a in range(4):
         for b in range(4):
             yy, xx = a * (1 - core) + b * core, b * (1 - core) + a * core
             wa[a, :, b] = wp[core, yy, :, xx] + wcore[yy, :, xx]
     first, second = y * (1 - core) + x * core, x * (1 - core) + y * core
-    r1, r2, r3 = [], [], []
-    for off in range(1, 4):
-        to = place.turn(y=off * (1 - core), x=off * core)[3]
-        r1.append(remote(wa.at[lax.rem(first + off, 4)], wr1.at[off - 1], off, to, rssend, rsrecv))
-        to = place.turn(y=off * core, x=off * (1 - core))[3]
-        r2.append(remote(wb_.at[lax.rem(second + off, 4)], wr2.at[off - 1], 3 + off, to, rssend, rsrecv))
-        zz, to = place.turn(z=off)[1::2]
-        r3.append(remote(wc.at[zz], wr3.at[off - 1], 6 + off, to, rssend, rsrecv))
-    r4 = [remote(wd, wr4, 10, place.sibling(), rssend, rsrecv)]
-    start(r1)
-    lax.fori_loop(BLOCKS // 2, BLOCKS, kgrad_step, 0)
+    to1 = [place.turn(y=off * (1 - core), x=off * core)[3] for off in range(1, 4)]
+    to2 = [place.turn(y=off * core, x=off * (1 - core))[3] for off in range(1, 4)]
+    to3 = [place.in_column(off) for off in range(1, 8)]
+    r1 = Stage(wr1, [(wa.at[lax.rem(first + 1 + n, 4)], wr1.at[n], p) for n, p in enumerate(to1)])
+    r2 = Stage(wr2, [(wb_.at[lax.rem(second + 1 + n, 4)], wr2.at[n], p) for n, p in enumerate(to2)])
+    r3 = Stage(wr3.reshape(8, 8, C).at[pl.ds(0, 7)], [(wc.at[zz], wr3.at[core, z], p) for zz, p in to3])
+    r1.start()
+    lax.fori_loop(CUT, BLOCKS, kgrad_step, 0)
 
     gain_g = jnp.sum(win * nsum, axis=1, keepdims=True)
     shift_g = jnp.sum(win * inb, axis=1, keepdims=True)
@@ -445,18 +450,17 @@
     for at, column in columns:
         grads = jnp.where(lane == at, column, grads)
     sp.reshape(128, C)[...] = grads * factor
-    q1, q2, q3 = [], [], []
+    q1, q2 = [], []
     for off in range(1, 8):
         g, to = place.in_plane(off)
-        q1.append(remote(sp.at[:, :, g // 2, lax.rem(g, 2)], srx.at[off - 1], 10 + off, to, rssend, rsrecv))
-    for off in range(1, 4):
-        yy, _, _, to = place.turn(y=off)
-        q2.append(remote(sb.at[yy], sry.at[off - 1], 17 + off, to, rssend, rsrecv))
-        zz, to = place.turn(z=off)[1::2]
-        q3.append(remote(sc.at[zz], srz.at[off - 1], 20 + off, to, rssend, rsrecv))
-    start(q1)
-
-    arrive(back[0:2])
+        q1.append((sp.at[:, :, g // 2, lax.rem(g, 2)], srx.at[off - 1], to))
+    for off in range(1, 16):
+        yy, zz, to = place.in_wall(off)
+        q2.append((sb.at[yy, zz], sry.at[off - 1], to))
+    q1, q2 = Stage(srx, q1), Stage(sry, q2)
+    q1.start()
+
+    back_side.arrive()
     clear_columns(place, dcv)
 
     def out_step(n, carry):
@@ -473,72 +477,80 @@
             fg[b, p, at, :] = acc[p]
         return carry
 
-    lax.fori_loop(0, 6, out_step, 0)
-    arrive(r1)
+    lax.fori_loop(0, 5, out_step, 0)
+    r1.arrive()
     for n in range(4):
         wb_[n] = wa[first, :, n] + wr1[0, :, n] + wr1[1, :, n] + wr1[2, :, n]
-    start(r2)
-    lax.fori_loop(6, 9, out_step, 0)
-    arrive(q1)
+    r2.start()
+    lax.fori_loop(5, 8, out_step, 0)
+    q1.arrive()
     total = sp[:, :, x, core]
     for n in range(7):
         total = total + srx[n]
     sb[...] = total
-    start(q2)
-    lax.fori_loop(9, 13, out_step, 0)
-    arrive(r2)
+    q2.start()
+    lax.fori_loop(8, 13, out_step, 0)
+    r2.arrive()
     wc[...] = wb_[second] + wr2[0] + wr2[1] + wr2[2]
-    start(r3)
-    arrive(q2)
-    sc[...] = sb[y] + sry[0] + sry[1] + sry[2]
-    start(q3)
+    r3.start()
+    wr3[core, z] = wc[z]
     lax.fori_loop(13, BLOCKS, out_step, 0)
-    arrive(back[2:])
+    back_ends.arrive()
     clear_rows(place, dcv)
     lax.fori_loop(0, BLOCKS, out_rest, 0)
     put = pltpu.make_async_copy(fg, fg_out, out_sem.at[0])
     put.start()
 
-    leave(s1 + w1 + v1 + s2 + w2 + v2 + s3 + w3 + v3 + edges + back + r0 + r1 + r2 + q1 + q2)
-    arrive(r3)
-    wd[...] = wc[z] + wr3[0] + wr3[1] + wr3[2]
-    start(r4)
-    arrive(q3)
-    small_out[...] = sc[z] + srz[0] + srz[1] + srz[2]
-    arrive(r4)
-    kept, got = wd[...], wr4[...]
-    weight_out[core] = jnp.where(core == 0, kept[0:4], kept[4:8])
-    weight_out[1 - core] = jnp.where(core == 0, got[0:4], got[4:8])
+    for stage in stages:
+        if stage not in (r3, q2):
+            stage.leave()
+    q2.arrive()
+    total = sb[y, z]
+    for n in range(15):
+        total = total + sry[n]
+    small_out[...] = total
+    r3.arrive()
+    for kind in range(2):
+        total = wr3[kind, 0] + wr3[kind, 1] + wr3[kind, 2] + wr3[kind, 3]
+        weight_out[kind] = jnp.where(core == 0, total[0:4], total[4:8])
 
     put.wait()
-    leave(r3 + r4 + q3)
+    r3.leave()
+    q2.leave()
 
 
 def deliver(
     fg_in, small_in, weight_in,
     fg_out, taps_out, cb_out, gain_out, shift_out, win_out, ib_out, wout_out, ob_out, scale_out,
-    buf, row, sem,
+    buf, row, weights, taps, cb, gain, shift, ib, ob, scale, sem,
 ):
     pieces = [(b, pl.ds(h, H // 2)) for b in range(B) for h in range(0, H, H // 2)]
     small = pltpu.make_async_copy(small_in, row, sem.at[8])
-    weights = [pltpu.make_async_copy(weight_in.at[k], ref, sem.at[9 + k]) for k, ref in enumerate((win_out, wout_out))]
-    small.start()
+    weight = pltpu.make_async_copy(weight_in, weights, sem.at[9])
     gets = [pltpu.make_async_copy(fg_in.at[at], buf.at[at], sem.at[n]) for n, at in enumerate(pieces)]
     puts = [pltpu.make_async_copy(buf.at[at], fg_out.at[at], sem.at[4 + n]) for n, at in enumerate(pieces)]
-    for copy in gets + weights:
+    for copy in [small, weight] + gets:
         copy.start()
     small.wait()
     for i in range(K):
         for j in range(K):
-            taps_out[i, 0, j] = row[0, TAPS + i * K + j]
-    for at, ref in ((CB, cb_out), (GAIN, gain_out), (SHIFT, shift_out), (OB, ob_out), (SCALE, scale_out)):
+            taps[i, 0, j] = row[0, TAPS + i * K + j]
+    for at, ref in ((CB, cb), (GAIN, gain), (SHIFT, shift), (OB, ob), (SCALE, scale)):
         ref[0] = row[0, at]
     for k in range(4):
-        ib_out[k] = row[0, IB + k]
+        ib[k] = row[0, IB + k]
+    ends = [
+        (taps, taps_out), (cb, cb_out), (gain, gain_out), (shift, shift_out), (ob, ob_out), (scale, scale_out),
+        (ib, ib_out), (weights.at[0], win_out), (weights.at[1], wout_out),
+    ]
+    weight.wait()
+    rest = [pltpu.make_async_copy(a, b, sem.at[10 + n]) for n, (a, b) in enumerate(ends)]
+    for copy in rest:
+        copy.start()
     for get, put in zip(gets, puts):
         get.wait()
         put.start()
-    for copy in weights + puts:
+    for copy in rest + puts:
         copy.wait()
 
 
@@ -553,7 +565,6 @@
     out = lambda *shape: jax.ShapeDtypeStruct(shape, f32)
     anywhere = pl.BlockSpec(memory_space=pl.ANY)
     inside = pl.BlockSpec(memory_space=pltpu.VMEM)
-    scalar = pl.BlockSpec(memory_space=pltpu.SMEM)
     tile = (B, H, W, C)
     fg, small, weights = pl.pallas_call(
         kernel,
@@ -567,9 +578,9 @@
             half(2 * C, HID), half(C, HID), half(HID, 2 * C), half(2 * C, HID), half(C, HID), vmem(1, HID),
             vmem(C, HID), vmem(C, HID), vmem(8, HID), vmem(K * K, 8, C), vmem(8, C), vmem(8, C),
             vmem(2, 4, 4, 4, 8, C), vmem(4, 4, 4, 8, C), vmem(4, 4, 4, 8, C), vmem(3, 4, 4, 8, C),
-            vmem(4, 4, 8, C), vmem(3, 4, 8, C), vmem(4, 8, C), vmem(3, 8, C), vmem(8, C), vmem(8, C),
-            vmem(128, C), vmem(4, 4, 4, 2, 1, C), vmem(7, 4, 4, 1, C), vmem(4, 4, 1, C), vmem(3, 4, 1, C), vmem(4, 1, C), vmem(3, 1, C),
-            dma(11), dma(1), dma(8), dma(8), dma(8), dma(8), dma(39), dma(39), dma(24), dma(24),
+            vmem(4, 4, 8, C), vmem(3, 4, 8, C), vmem(4, 8, C), vmem(2, 4, 8, C),
+            vmem(128, C), vmem(4, 4, 4, 2, 1, C), vmem(7, 4, 4, 1, C), vmem(4, 4, 1, C), vmem(15, 1, C),
+            dma(11), dma(1), dma(18), dma(18),
         ],
         compiler_params=pltpu.CompilerParams(
             collective_id=0, has_side_effects=True, vmem_limit_bytes=56 * 2**20
@@ -584,8 +595,10 @@
             out(*tile), out(K, 1, K), out(1), out(1), out(1), out(4, C), out(4), out(4, C), out(1), out(1),
         ),
         in_specs=[anywhere] * 3,
-        out_specs=(anywhere, scalar, scalar, scalar, scalar, inside, scalar, inside, scalar, scalar),
-        scratch_shapes=[vmem(*tile), smem(1, C), dma(11)],
+        out_specs=(anywhere,) * 10,
+        scratch_shapes=[
+            vmem(*tile), smem(1, C), vmem(2, 4, C), smem(K, 1, K), smem(1), smem(1), smem(1), smem(4), smem(1), smem(1), dma(19),
+        ],
     )(fg, small, weights)
     return fg, taps_g.transpose(0, 2, 1), cb_g, gain_g, shift_g, win_g.T, ib_g, wout_g, ob_g, scale_g
 

time: 58.8 us -> 57.1 us (0.971)
  Pallas kernels: 54.7 us -> 53.1 us
    pallas_call x1, Pallas kernels: 52.1 us -> 51 us  [per_device(): pl.pallas_call(kernel, out_shape=(out(*tile), out(1, C), out(2, 4, C)), i...]
where the time goes in v4:
time: 57.1 us; the launch traced here: 56.9 us
  Pallas kernels  53.1 us (93%)
  between operations  3.88 us (7%)
    pallas_call x1, Pallas kernels, per_device(): pl.pallas_call(kernel, out_shape=(out(*tile), out(1, C), out(2, 4, C)), i...  51 us
    pallas_call x1, Pallas kernels, per_device(): pl.pallas_call(deliver, out_shape=(out(*tile), out(K, 1, K), out(1), out(...  2.09 us

profile of v4, /device:TPU:1, one launch (start us, length us, event | category | flops | bytes accessed | tf_op | source)
XLA Modules:
  0.0 56.9 jit_solution(4004378880558420660)
XLA Ops:
  3.9 51.0 %shard_map.186 = (f32[2,16,64,128]{3,2,1,0:T(8,128)}, f32[1,128]{1,0:T(1,128)}, f32[2,4,128]{2,1,0:T(4,128)}) custom-call(f32[2,16,64,128]{3,2,1,0:T(8,128)} %feat.1, f32[2,16,64,128]{3,2,1,0:T(8,128)} %cot_hbm.1, f32[7,1,7]{2,1,0:T(1,128)} %bitcast.4, f32[1]{0:T(128)S(6)} %copy.21.cb_in, f32[1]{0:T(128)S(6)} %copy.22.gain_in, f32[1]{0:T(128)S(6)} %copy.23.shift_in, ...), custom_call_target="tpu_custom_call" | custom-call | tf_op jit(solution)/shard_map/pallas_call | solution.py:569
  54.9 2.1 %shard_map.187 = (f32[2,16,64,128]{3,2,1,0:T(8,128)}, f32[7,1,7]{2,1,0:T(1,128)}, f32[1]{0:T(128)}, f32[1]{0:T(128)}, f32[1]{0:T(128)}, /*index=5*/f32[4,128]{1,...) custom-call(f32[2,16,64,128]{3,2,1,0:T(8,128)} %get-tuple-element.23.fg_in, ...), custom_call_target="tpu_custom_call" | custom-call | tf_op jit(solution)/shard_map/pallas_call | solution.py:592

commit v5 on v4

--- a/solution.py
+++ b/solution.py
@@ -97,8 +97,8 @@
 def edge_ends(place, src, row0, col0, ext):
     return [
         (
-            src.at[:, rows_of(dr, row0, True), cols_of(dc, col0, True), :],
-            ext.at[:, rows_of(dr, R, False), cols_of(dc, LEFT, False), :],
+            src.at[rows_of(dr, row0, True), cols_of(dc, col0, True), :],
+            ext.at[rows_of(dr, R, False), cols_of(dc, LEFT, False), :],
             place.neighbour(dr, dc),
         )
         for dr, dc in STEPS
@@ -248,27 +248,37 @@
 
     cell = (y, z, x, core)
     plane = [place.in_plane(off)[1] for off in range(1, 8)]
-    column = [place.in_column(off)[1] for off in range(1, 8)]
+    zs = [place.turn(z=off)[3] for off in range(1, 4)]
     wall = [place.in_wall(off)[2] for off in range(1, 16)]
     xs = [place.turn(x=off)[3] for off in range(1, 4)]
     ys = [place.turn(y=off)[3] for off in range(1, 4)]
     cells = wg.at[0].reshape(128, 4, C)
     s1 = Stage(srx.at[:, 0, 0], [(srow, sg.at[cell], p) for p in plane])
-    w1 = Stage(cells.at[pl.ds(0, 7)], [(win_in, wg.at[(0, *cell)], p) for p in column])
-    v1 = Stage(cells.at[pl.ds(0, 7)], [(wout_in, wg.at[(1, *cell)], p) for p in column])
+    w1 = Stage(cells.at[pl.ds(0, 3)], [(win_in, wg.at[(0, *cell)], p) for p in zs])
+    v1 = Stage(cells.at[pl.ds(0, 3)], [(wout_in, wg.at[(1, *cell)], p) for p in zs])
     s2 = Stage(sg.reshape(128, 1, C).at[pl.ds(0, 120)], [(sg.at[y, z], sg.at[y, z], p) for p in wall])
-    w2 = Stage(cells.at[pl.ds(0, 24)], [(wg.at[0, y, :, x], wg.at[0, y, :, x], p) for p in xs])
-    v2 = Stage(cells.at[pl.ds(0, 24)], [(wg.at[1, y, :, x], wg.at[1, y, :, x], p) for p in ys])
-    w3 = Stage(cells.at[pl.ds(0, 96)], [(wg.at[0, y], wg.at[0, y], p) for p in ys])
-    v3 = Stage(cells.at[pl.ds(0, 96)], [(wg.at[1, :, :, x], wg.at[1, :, :, x], p) for p in xs])
-    edges = edge_ends(place, feat, 0, 0, src)
-    side = Stage(src.at[:, pl.ds(0, H), pl.ds(0, 2 * LEFT), :], edges[0:2])
-    ends = Stage(src.at[:, pl.ds(0, 2 * R), :, :], edges[2:])
+    part = wg.at[0, y, :, x, core]
+    w2 = Stage(cells.at[pl.ds(0, 12)], [(part, part, p) for p in xs])
+    other = wg.at[1, y, :, x, core]
+    v2 = Stage(cells.at[pl.ds(0, 12)], [(other, other, p) for p in ys])
+    layer = wg.at[0, y, :, :, core]
+    w3 = Stage(cells.at[pl.ds(0, 48)], [(layer, layer, p) for p in ys])
+    slab = wg.at[1, :, :, x, core]
+    v3 = Stage(cells.at[pl.ds(0, 48)], [(slab, slab, p) for p in xs])
+    lot = wg.at[:, :, :, :, core]
+    w4 = Stage(cells, [(lot, lot, place.sibling())])
+    def tile_edges(b, ref, row0, col0, ext):
+        edges = edge_ends(place, ref.at[b], row0, col0, ext.at[b])
+        sides = Stage(src.at[b, pl.ds(0, H), pl.ds(0, 2 * LEFT), :], edges[0:2])
+        return sides, Stage(src.at[b, pl.ds(0, 2 * R), :, :], edges[2:])
+
+    (side0, ends0), (side1, ends1) = (tile_edges(b, feat, 0, 0, src) for b in range(B))
 
     s1.start()
     w1.start()
     v1.start()
-    side.start()
+    side0.start()
+    side1.start()
     own[2].wait()
     own[3].wait()
     s1.arrive()
@@ -277,14 +287,16 @@
     w2.start()
     v1.arrive()
     v2.start()
-    ends.start()
+    ends0.start()
+    ends1.start()
     w2.arrive()
     w3.start()
     v2.arrive()
     v3.start()
     own[0].wait()
     own[1].wait()
-    side.arrive()
+    side0.arrive()
+    side1.arrive()
     clear_columns(place, src)
     s2.arrive()
 
@@ -304,7 +316,11 @@
             mid[b, p, at, :] = acc[p]
         return carry
 
-    lax.fori_loop(0, BLOCKS, conv_step, 0)
+    lax.fori_loop(0, BLOCKS // 2, conv_step, 0)
+    w3.arrive()
+    v3.arrive()
+    w4.start()
+    lax.fori_loop(BLOCKS // 2, BLOCKS, conv_step, 0)
 
     def conv_rest(n, carry):
         b, wb, at = column_block(n)
@@ -313,8 +329,7 @@
             mid[b, p, at, :] = acc[p]
         return carry
 
-    w3.arrive()
-    v3.arrive()
+    w4.arrive()
     gain_wide, shift_wide = widen(small[:, GAIN : GAIN + 1], 4), widen(small[:, SHIFT : SHIFT + 1], 4)
     scale_wide, ob_wide = widen(small[:, SCALE : SCALE + 1], 4), widen(small[:, OB : OB + 1], 1)
     win_t = wg.at[0].reshape(HID, C)[...]
@@ -381,28 +396,32 @@
             part = dc[n * (M // 2) : (n + 1) * (M // 2)]
             dcv[b, pl.ds(R + p, QUARTER), LEFT : LEFT + W, :] = part.reshape(QUARTER, W, C)
 
-    back = edge_ends(place, dcv, R, LEFT, dcv)
-    back_side = Stage(src.at[:, pl.ds(0, H), pl.ds(0, 2 * LEFT), :], back[0:2])
-    back_ends = Stage(src.at[:, pl.ds(0, 2 * R), :, :], back[2:])
+    (back_side0, back_ends0), (back_side1, back_ends1) = (tile_edges(b, dcv, R, LEFT, dcv) for b in range(B))
 
     def mix_step(n, carry):
         outer = lax.rem((n + 1) // 2, 2)
 
         @pl.when(n == 1)
         def _():
-            ends.arrive()
+            ends0.arrive()
+            ends1.arrive()
             clear_rows(place, src)
             lax.fori_loop(0, BLOCKS, conv_rest, 0)
 
+        @pl.when(n == 2)
+        def _():
+            back_ends0.start()
+            back_side0.start()
+
         @pl.when(n == 3)
         def _():
-            back_ends.start()
+            back_ends1.start()
 
         mix(n // 2, (QUARTER * (1 - outer), QUARTER * (2 + outer)))
         return carry
 
     lax.fori_loop(0, 4, mix_step, 0)
-    back_side.start()
+    back_side1.start()
 
     factor = 1.0 / math.sqrt(B * H * W * ROWS * COLS)
     nsum, msum = nacc[...], macc[...]
@@ -460,7 +479,8 @@
     q1, q2 = Stage(srx, q1), Stage(sry, q2)
     q1.start()
 
-    back_side.arrive()
+    back_side0.arrive()
+    back_side1.arrive()
     clear_columns(place, dcv)
 
     def out_step(n, carry):
@@ -495,7 +515,8 @@
     r3.start()
     wr3[core, z] = wc[z]
     lax.fori_loop(13, BLOCKS, out_step, 0)
-    back_ends.arrive()
+    back_ends0.arrive()
+    back_ends1.arrive()
     clear_rows(place, dcv)
     lax.fori_loop(0, BLOCKS, out_rest, 0)
     put = pltpu.make_async_copy(fg, fg_out, out_sem.at[0])
@@ -580,7 +601,7 @@
             vmem(2, 4, 4, 4, 8, C), vmem(4, 4, 4, 8, C), vmem(4, 4, 4, 8, C), vmem(3, 4, 4, 8, C),
             vmem(4, 4, 8, C), vmem(3, 4, 8, C), vmem(4, 8, C), vmem(2, 4, 8, C),
             vmem(128, C), vmem(4, 4, 4, 2, 1, C), vmem(7, 4, 4, 1, C), vmem(4, 4, 1, C), vmem(15, 1, C),
-            dma(11), dma(1), dma(18), dma(18),
+            dma(11), dma(1), dma(23), dma(23),
         ],
         compiler_params=pltpu.CompilerParams(
             collective_id=0, has_side_effects=True, vmem_limit_bytes=56 * 2**20

time: 57.1 us -> 55.5 us (0.972)
  Pallas kernels: 53.1 us -> 51.5 us
    pallas_call x1, Pallas kernels: 51 us -> 49.4 us  [per_device(): pl.pallas_call(kernel, out_shape=(out(*tile), out(1, C), out(2, 4, C)), i...]
where the time goes in v5:
time: 55.5 us; the launch traced here: 55.3 us
  Pallas kernels  51.5 us (93%)
  between operations  3.88 us (7%)
    pallas_call x1, Pallas kernels, per_device(): pl.pallas_call(kernel, out_shape=(out(*tile), out(1, C), out(2, 4, C)), i...  49.4 us
    pallas_call x1, Pallas kernels, per_device(): pl.pallas_call(deliver, out_shape=(out(*tile), out(K, 1, K), out(1), out(...  2.09 us

profile of v5, /device:TPU:1, one launch (start us, length us, event | category | flops | bytes accessed | tf_op | source)
XLA Modules:
  0.0 55.3 jit_solution(8601861515682040229)
XLA Ops:
  3.9 49.4 %shard_map.186 = (f32[2,16,64,128]{3,2,1,0:T(8,128)}, f32[1,128]{1,0:T(1,128)}, f32[2,4,128]{2,1,0:T(4,128)}) custom-call(f32[2,16,64,128]{3,2,1,0:T(8,128)} %feat.1, f32[2,16,64,128]{3,2,1,0:T(8,128)} %cot_hbm.1, f32[7,1,7]{2,1,0:T(1,128)} %bitcast.4, f32[1]{0:T(128)S(6)} %copy.21.cb_in, f32[1]{0:T(128)S(6)} %copy.22.gain_in, f32[1]{0:T(128)S(6)} %copy.23.shift_in, ...), custom_call_target="tpu_custom_call" | custom-call | tf_op jit(solution)/shard_map/pallas_call | solution.py:590
  53.3 2.1 %shard_map.187 = (f32[2,16,64,128]{3,2,1,0:T(8,128)}, f32[7,1,7]{2,1,0:T(1,128)}, f32[1]{0:T(128)}, f32[1]{0:T(128)}, f32[1]{0:T(128)}, /*index=5*/f32[4,128]{1,...) custom-call(f32[2,16,64,128]{3,2,1,0:T(8,128)} %get-tuple-element.23.fg_in, ...), custom_call_target="tpu_custom_call" | custom-call | tf_op jit(solution)/shard_map/pallas_call | solution.py:613

commit v6 on v5

--- a/solution.py
+++ b/solution.py
@@ -24,6 +24,7 @@
 QUARTER = H // 4
 BLOCKS = B * W // 8
 CUT = BLOCKS // 2 + 1
+LATE = BLOCKS - 5
 M = 2 * QUARTER * W
 TAPS, CB, GAIN, SHIFT, OB, SCALE, IB = 0, 49, 50, 51, 52, 53, 54
 
@@ -75,34 +76,36 @@
         return (lax.rem(self.row + dr + ROWS, ROWS), lax.rem(self.col + dc + COLS, COLS))
 
 
-STEPS = [(0, -1), (0, 1), (-1, 0), (1, 0), (-1, -1), (-1, 1), (1, -1), (1, 1)]
-
-
-def rows_of(step, base, sent):
-    if step == 0:
-        return pl.ds(base, H)
-    if sent:
-        return pl.ds(base, R) if step < 0 else pl.ds(base + H - R, R)
-    return pl.ds(R + H, R) if step < 0 else pl.ds(0, R)
-
-
-def cols_of(step, base, sent):
-    if step == 0:
-        return pl.ds(base, W)
-    if sent:
-        return pl.ds(base, LEFT) if step < 0 else pl.ds(base + W - LEFT, LEFT)
-    return pl.ds(LEFT + W, LEFT) if step < 0 else pl.ds(0, LEFT)
-
-
-def edge_ends(place, src, row0, col0, ext):
-    return [
-        (
-            src.at[rows_of(dr, row0, True), cols_of(dc, col0, True), :],
-            ext.at[rows_of(dr, R, False), cols_of(dc, LEFT, False), :],
-            place.neighbour(dr, dc),
+def side_ends(place, src, row0, col0, ext):
+    ends = []
+    for dc in (-1, 1):
+        read = col0 if dc < 0 else col0 + W - LEFT
+        land = LEFT + W if dc < 0 else 0
+        ends.append(
+            (
+                src.at[pl.ds(row0, H), pl.ds(read, LEFT), :],
+                ext.at[pl.ds(R, H), pl.ds(land, LEFT), :],
+                place.neighbour(0, dc),
+            )
         )
-        for dr, dc in STEPS
-    ]
+    return ends
+
+
+def row_ends(place, src, row0, col0, ext, near):
+    odd = lax.rem(place.row, 2)
+    low = odd if near else 1 - odd
+    rows, landing = pl.ds(row0 + (H - R) * (1 - low), R), pl.ds((R + H) * low, R)
+    ends = []
+    for dc in (0, -1, 1):
+        read, land, n = (col0, LEFT, W) if dc == 0 else (col0, LEFT + W, LEFT) if dc < 0 else (col0 + W - LEFT, 0, LEFT)
+        ends.append(
+            (
+                src.at[rows, pl.ds(read, n), :],
+                ext.at[landing, pl.ds(land, n), :],
+                place.neighbour(1 - 2 * low, dc),
+            )
+        )
+    return ends
 
 
 def clear_columns(place, ext):
@@ -192,7 +195,7 @@
         copy.start()
 
     barrier = pltpu.get_barrier_semaphore()
-    partners = [place.neighbour(dr, dc) for dr, dc in STEPS]
+    partners = [place.neighbour(dr, dc) for dr in (-1, 0, 1) for dc in (-1, 0, 1) if dr or dc]
     partners += [place.in_plane(off)[1] for off in range(1, 8)]
     partners += [place.in_column(off)[1] for off in range(1, 8)]
     partners += [place.in_wall(off)[2] for off in range(1, 16)]
@@ -267,18 +270,29 @@
     v3 = Stage(cells.at[pl.ds(0, 48)], [(slab, slab, p) for p in xs])
     lot = wg.at[:, :, :, :, core]
     w4 = Stage(cells, [(lot, lot, place.sibling())])
-    def tile_edges(b, ref, row0, col0, ext):
-        edges = edge_ends(place, ref.at[b], row0, col0, ext.at[b])
-        sides = Stage(src.at[b, pl.ds(0, H), pl.ds(0, 2 * LEFT), :], edges[0:2])
-        return sides, Stage(src.at[b, pl.ds(0, 2 * R), :, :], edges[2:])
-
-    (side0, ends0), (side1, ends1) = (tile_edges(b, feat, 0, 0, src) for b in range(B))
+    def tile_edges(ref, row0, col0, ext):
+        sides, nears, fars = [], [], []
+        for b in range(B):
+            ends = (place, ref.at[b], row0, col0, ext.at[b])
+            sides.append(Stage(src.at[b, pl.ds(0, H), pl.ds(0, 2 * LEFT), :], side_ends(*ends)))
+            nears.append(Stage(src.at[b, pl.ds(0, R), :, :], row_ends(*ends, True)))
+            fars.append(Stage(src.at[b, pl.ds(0, R), :, :], row_ends(*ends, False)))
+        return sides, nears, fars
+
+    def start(*stages):
+        for stage in stages:
+            stage.start()
+
+    def arrive(*stages):
+        for stage in stages:
+            stage.arrive()
+
+    sides, nears, fars = tile_edges(feat, 0, 0, src)
 
     s1.start()
     w1.start()
     v1.start()
-    side0.start()
-    side1.start()
+    start(*sides)
     own[2].wait()
     own[3].wait()
     s1.arrive()
@@ -287,16 +301,15 @@
     w2.start()
     v1.arrive()
     v2.start()
-    ends0.start()
-    ends1.start()
+    start(*nears)
     w2.arrive()
     w3.start()
     v2.arrive()
     v3.start()
+    start(*fars)
     own[0].wait()
     own[1].wait()
-    side0.arrive()
-    side1.arrive()
+    arrive(*sides)
     clear_columns(place, src)
     s2.arrive()
 
@@ -316,11 +329,11 @@
             mid[b, p, at, :] = acc[p]
         return carry
 
-    lax.fori_loop(0, BLOCKS // 2, conv_step, 0)
+    lax.fori_loop(0, LATE, conv_step, 0)
     w3.arrive()
     v3.arrive()
     w4.start()
-    lax.fori_loop(BLOCKS // 2, BLOCKS, conv_step, 0)
+    lax.fori_loop(LATE, BLOCKS, conv_step, 0)
 
     def conv_rest(n, carry):
         b, wb, at = column_block(n)
@@ -396,32 +409,30 @@
             part = dc[n * (M // 2) : (n + 1) * (M // 2)]
             dcv[b, pl.ds(R + p, QUARTER), LEFT : LEFT + W, :] = part.reshape(QUARTER, W, C)
 
-    (back_side0, back_ends0), (back_side1, back_ends1) = (tile_edges(b, dcv, R, LEFT, dcv) for b in range(B))
+    back_sides, back_nears, back_fars = tile_edges(dcv, R, LEFT, dcv)
 
     def mix_step(n, carry):
         outer = lax.rem((n + 1) // 2, 2)
 
         @pl.when(n == 1)
         def _():
-            ends0.arrive()
-            ends1.arrive()
+            arrive(*nears, *fars)
             clear_rows(place, src)
             lax.fori_loop(0, BLOCKS, conv_rest, 0)
 
         @pl.when(n == 2)
         def _():
-            back_ends0.start()
-            back_side0.start()
+            start(back_fars[0], back_nears[0], back_sides[0])
 
         @pl.when(n == 3)
         def _():
-            back_ends1.start()
+            start(back_fars[1], back_nears[1])
 
         mix(n // 2, (QUARTER * (1 - outer), QUARTER * (2 + outer)))
         return carry
 
     lax.fori_loop(0, 4, mix_step, 0)
-    back_side1.start()
+    back_sides[1].start()
 
     factor = 1.0 / math.sqrt(B * H * W * ROWS * COLS)
     nsum, msum = nacc[...], macc[...]
@@ -438,15 +449,10 @@
     lax.fori_loop(0, CUT, kgrad_step, 0)
     r0.arrive()
     for a in range(4):
-        for b in range(4):
-            yy, xx = a * (1 - core) + b * core, b * (1 - core) + a * core
-            wa[a, :, b] = wp[core, yy, :, xx] + wcore[yy, :, xx]
-    first, second = y * (1 - core) + x * core, x * (1 - core) + y * core
-    to1 = [place.turn(y=off * (1 - core), x=off * core)[3] for off in range(1, 4)]
-    to2 = [place.turn(y=off * core, x=off * (1 - core))[3] for off in range(1, 4)]
+        wa[a] = wp[core, :, :, a] + wcore[:, :, a]
     to3 = [place.in_column(off) for off in range(1, 8)]
-    r1 = Stage(wr1, [(wa.at[lax.rem(first + 1 + n, 4)], wr1.at[n], p) for n, p in enumerate(to1)])
-    r2 = Stage(wr2, [(wb_.at[lax.rem(second + 1 + n, 4)], wr2.at[n], p) for n, p in enumerate(to2)])
+    r1 = Stage(wr1, [(wa.at[lax.rem(x + 1 + n, 4)], wr1.at[n], p) for n, p in enumerate(xs)])
+    r2 = Stage(wr2, [(wb_.at[lax.rem(y + 1 + n, 4)], wr2.at[n], p) for n, p in enumerate(ys)])
     r3 = Stage(wr3.reshape(8, 8, C).at[pl.ds(0, 7)], [(wc.at[zz], wr3.at[core, z], p) for zz, p in to3])
     r1.start()
     lax.fori_loop(CUT, BLOCKS, kgrad_step, 0)
@@ -479,8 +485,7 @@
     q1, q2 = Stage(srx, q1), Stage(sry, q2)
     q1.start()
 
-    back_side0.arrive()
-    back_side1.arrive()
+    arrive(*back_sides)
     clear_columns(place, dcv)
 
     def out_step(n, carry):
@@ -499,8 +504,7 @@
 
     lax.fori_loop(0, 5, out_step, 0)
     r1.arrive()
-    for n in range(4):
-        wb_[n] = wa[first, :, n] + wr1[0, :, n] + wr1[1, :, n] + wr1[2, :, n]
+    wb_[...] = wa[x] + wr1[0] + wr1[1] + wr1[2]
     r2.start()
     lax.fori_loop(5, 8, out_step, 0)
     q1.arrive()
@@ -511,12 +515,11 @@
     q2.start()
     lax.fori_loop(8, 13, out_step, 0)
     r2.arrive()
-    wc[...] = wb_[second] + wr2[0] + wr2[1] + wr2[2]
+    wc[...] = wb_[y] + wr2[0] + wr2[1] + wr2[2]
     r3.start()
     wr3[core, z] = wc[z]
     lax.fori_loop(13, BLOCKS, out_step, 0)
-    back_ends0.arrive()
-    back_ends1.arrive()
+    arrive(*back_nears, *back_fars)
     clear_rows(place, dcv)
     lax.fori_loop(0, BLOCKS, out_rest, 0)
     put = pltpu.make_async_copy(fg, fg_out, out_sem.at[0])
@@ -601,7 +604,7 @@
             vmem(2, 4, 4, 4, 8, C), vmem(4, 4, 4, 8, C), vmem(4, 4, 4, 8, C), vmem(3, 4, 4, 8, C),
             vmem(4, 4, 8, C), vmem(3, 4, 8, C), vmem(4, 8, C), vmem(2, 4, 8, C),
             vmem(128, C), vmem(4, 4, 4, 2, 1, C), vmem(7, 4, 4, 1, C), vmem(4, 4, 1, C), vmem(15, 1, C),
-            dma(11), dma(1), dma(23), dma(23),
+            dma(11), dma(1), dma(27), dma(27),
         ],
         compiler_params=pltpu.CompilerParams(
             collective_id=0, has_side_effects=True, vmem_limit_bytes=56 * 2**20

time: 55.5 us -> 55.7 us (level)
  no operation moved by 1% of the time
where the time goes in v6:
time: 55.7 us; the launch traced here: 55.5 us
  Pallas kernels  51.6 us (93%)
  between operations  3.88 us (7%)
    pallas_call x1, Pallas kernels, per_device(): pl.pallas_call(kernel, out_shape=(out(*tile), out(1, C), out(2, 4, C)), i...  49.5 us
    pallas_call x1, Pallas kernels, per_device(): pl.pallas_call(deliver, out_shape=(out(*tile), out(K, 1, K), out(1), out(...  2.09 us

profile of v6, /device:TPU:1, one launch (start us, length us, event | category | flops | bytes accessed | tf_op | source)
XLA Modules:
  0.0 55.5 jit_solution(18139489072563122551)
XLA Ops:
  3.9 49.5 %shard_map.186 = (f32[2,16,64,128]{3,2,1,0:T(8,128)}, f32[1,128]{1,0:T(1,128)}, f32[2,4,128]{2,1,0:T(4,128)}) custom-call(f32[2,16,64,128]{3,2,1,0:T(8,128)} %feat.1, f32[2,16,64,128]{3,2,1,0:T(8,128)} %cot_hbm.1, f32[7,1,7]{2,1,0:T(1,128)} %bitcast.4, f32[1]{0:T(128)S(6)} %copy.21.cb_in, f32[1]{0:T(128)S(6)} %copy.22.gain_in, f32[1]{0:T(128)S(6)} %copy.23.shift_in, ...), custom_call_target="tpu_custom_call" | custom-call | tf_op jit(solution)/shard_map/pallas_call | solution.py:593
  53.4 2.1 %shard_map.187 = (f32[2,16,64,128]{3,2,1,0:T(8,128)}, f32[7,1,7]{2,1,0:T(1,128)}, f32[1]{0:T(128)}, f32[1]{0:T(128)}, f32[1]{0:T(128)}, /*index=5*/f32[4,128]{1,...) custom-call(f32[2,16,64,128]{3,2,1,0:T(8,128)} %get-tuple-element.23.fg_in, ...), custom_call_target="tpu_custom_call" | custom-call | tf_op jit(solution)/shard_map/pallas_call | solution.py:616

commit v7 on v6

--- a/solution.py
+++ b/solution.py
@@ -108,14 +108,14 @@
     return ends
 
 
-def clear_columns(place, ext):
+def clear_columns(place, ext, b):
     @pl.when(place.col == 0)
     def _():
-        ext[:, R : R + H, 0:LEFT] = jnp.zeros((B, H, LEFT, C), f32)
+        ext[b, R : R + H, 0:LEFT] = jnp.zeros((H, LEFT, C), f32)
 
     @pl.when(place.col == COLS - 1)
     def _():
-        ext[:, R : R + H, LEFT + W :] = jnp.zeros((B, H, LEFT, C), f32)
+        ext[b, R : R + H, LEFT + W :] = jnp.zeros((H, LEFT, C), f32)
 
 
 def clear_rows(place, ext):
@@ -310,7 +310,8 @@
     own[0].wait()
     own[1].wait()
     arrive(*sides)
-    clear_columns(place, src)
+    clear_columns(place, src, 0)
+    clear_columns(place, src, 1)
     s2.arrive()
 
     small = sg.reshape(128, C)[...]
@@ -412,27 +413,23 @@
     back_sides, back_nears, back_fars = tile_edges(dcv, R, LEFT, dcv)
 
     def mix_step(n, carry):
-        outer = lax.rem((n + 1) // 2, 2)
-
-        @pl.when(n == 1)
+        outer = n // 2
+
+        @pl.when(n == 2)
         def _():
             arrive(*nears, *fars)
             clear_rows(place, src)
             lax.fori_loop(0, BLOCKS, conv_rest, 0)
 
-        @pl.when(n == 2)
+        @pl.when(n == 3)
         def _():
             start(back_fars[0], back_nears[0], back_sides[0])
 
-        @pl.when(n == 3)
-        def _():
-            start(back_fars[1], back_nears[1])
-
-        mix(n // 2, (QUARTER * (1 - outer), QUARTER * (2 + outer)))
+        mix(lax.rem(n, 2), (QUARTER * (1 - outer), QUARTER * (2 + outer)))
         return carry
 
     lax.fori_loop(0, 4, mix_step, 0)
-    back_sides[1].start()
+    start(back_fars[1], back_nears[1])
 
     factor = 1.0 / math.sqrt(B * H * W * ROWS * COLS)
     nsum, msum = nacc[...], macc[...]
@@ -455,6 +452,7 @@
     r2 = Stage(wr2, [(wb_.at[lax.rem(y + 1 + n, 4)], wr2.at[n], p) for n, p in enumerate(ys)])
     r3 = Stage(wr3.reshape(8, 8, C).at[pl.ds(0, 7)], [(wc.at[zz], wr3.at[core, z], p) for zz, p in to3])
     r1.start()
+    back_sides[1].start()
     lax.fori_loop(CUT, BLOCKS, kgrad_step, 0)
 
     gain_g = jnp.sum(win * nsum, axis=1, keepdims=True)
@@ -485,8 +483,8 @@
     q1, q2 = Stage(srx, q1), Stage(sry, q2)
     q1.start()
 
-    arrive(*back_sides)
-    clear_columns(place, dcv)
+    back_sides[0].arrive()
+    clear_columns(place, dcv, 0)
 
     def out_step(n, carry):
         b, wb, at = column_block(n)
@@ -513,6 +511,8 @@
         total = total + srx[n]
     sb[...] = total
     q2.start()
+    back_sides[1].arrive()
+    clear_columns(place, dcv, 1)
     lax.fori_loop(8, 13, out_step, 0)
     r2.arrive()
     wc[...] = wb_[y] + wr2[0] + wr2[1] + wr2[2]

time: 55.7 us -> 55.3 us (level)
  no operation moved by 1% of the time
where the time goes in v7:
time: 55.3 us; the launch traced here: 55.1 us
  Pallas kernels  51.2 us (93%)
  between operations  3.88 us (7%)
    pallas_call x1, Pallas kernels, per_device(): pl.pallas_call(kernel, out_shape=(out(*tile), out(1, C), out(2, 4, C)), i...  49.2 us
    pallas_call x1, Pallas kernels, per_device(): pl.pallas_call(deliver, out_shape=(out(*tile), out(K, 1, K), out(1), out(...  2.09 us

profile of v7, /device:TPU:1, one launch (start us, length us, event | category | flops | bytes accessed | tf_op | source)
XLA Modules:
  0.0 55.1 jit_solution(14605018650263320068)
XLA Ops:
  3.9 49.2 %shard_map.186 = (f32[2,16,64,128]{3,2,1,0:T(8,128)}, f32[1,128]{1,0:T(1,128)}, f32[2,4,128]{2,1,0:T(4,128)}) custom-call(f32[2,16,64,128]{3,2,1,0:T(8,128)} %feat.1, f32[2,16,64,128]{3,2,1,0:T(8,128)} %cot_hbm.1, f32[7,1,7]{2,1,0:T(1,128)} %bitcast.4, f32[1]{0:T(128)S(6)} %copy.21.cb_in, f32[1]{0:T(128)S(6)} %copy.22.gain_in, f32[1]{0:T(128)S(6)} %copy.23.shift_in, ...), custom_call_target="tpu_custom_call" | custom-call | tf_op jit(solution)/shard_map/pallas_call | solution.py:593
  53.0 2.1 %shard_map.187 = (f32[2,16,64,128]{3,2,1,0:T(8,128)}, f32[7,1,7]{2,1,0:T(1,128)}, f32[1]{0:T(128)}, f32[1]{0:T(128)}, f32[1]{0:T(128)}, /*index=5*/f32[4,128]{1,...) custom-call(f32[2,16,64,128]{3,2,1,0:T(8,128)} %get-tuple-element.23.fg_in, ...), custom_call_target="tpu_custom_call" | custom-call | tf_op jit(solution)/shard_map/pallas_call | solution.py:616

commit v8 on v7

--- a/solution.py
+++ b/solution.py
@@ -61,9 +61,9 @@
         other = lax.rem(self.g + off, 8)
         return other, self.at(self.y, self.z, other // 2, lax.rem(other, 2))
 
-    def in_column(self, off):
-        other = lax.rem(self.z * 2 + self.core + off, 8)
-        return other // 2, self.at(self.y, other // 2, self.x, lax.rem(other, 2))
+    def in_slab(self, off):
+        y, z = lax.rem(self.y + off // 8, 4), lax.rem(self.z + off // 2 % 4, 4)
+        return y, z, self.at(y, z, self.x, lax.rem(self.core + off, 2))
 
     def in_wall(self, off):
         y, z = lax.rem(self.y + off // 4, 4), lax.rem(self.z + off % 4, 4)
@@ -177,7 +177,7 @@
     src, cot, dcv, mid, fg, sg, wg, taps,
     win2, winlo, wintop, wot2, wotlo, bias_eff,
     nacc, macc, inbacc, kacc, cotacc, dbacc,
-    wp, wcore, wa, wr1, wb_, wr2, wc, wr3, rows, sp, srx, sb, sry,
+    wp, wcore, wa, wr1, wb_, wr2, rows, sp, srx, sb, sry,
     local, out_sem, sent, arrived,
 ):
     place = Place()
@@ -197,8 +197,7 @@
     barrier = pltpu.get_barrier_semaphore()
     partners = [place.neighbour(dr, dc) for dr in (-1, 0, 1) for dc in (-1, 0, 1) if dr or dc]
     partners += [place.in_plane(off)[1] for off in range(1, 8)]
-    partners += [place.in_column(off)[1] for off in range(1, 8)]
-    partners += [place.in_wall(off)[2] for off in range(1, 16)]
+    partners += [place.in_slab(off)[2] for off in range(1, 32)]
     for partner in partners:
         pl.semaphore_signal(barrier, inc=1, device_id=partner, device_id_type=MESH)
 
@@ -447,10 +446,9 @@
     r0.arrive()
     for a in range(4):
         wa[a] = wp[core, :, :, a] + wcore[:, :, a]
-    to3 = [place.in_column(off) for off in range(1, 8)]
+    slab = [place.in_slab(off) for off in range(1, 32)]
     r1 = Stage(wr1, [(wa.at[lax.rem(x + 1 + n, 4)], wr1.at[n], p) for n, p in enumerate(xs)])
-    r2 = Stage(wr2, [(wb_.at[lax.rem(y + 1 + n, 4)], wr2.at[n], p) for n, p in enumerate(ys)])
-    r3 = Stage(wr3.reshape(8, 8, C).at[pl.ds(0, 7)], [(wc.at[zz], wr3.at[core, z], p) for zz, p in to3])
+    r2 = Stage(wr2.reshape(32, 8, C).at[pl.ds(0, 31)], [(wb_.at[yy, zz], wr2.at[core, y, z], p) for yy, zz, p in slab])
     r1.start()
     back_sides[1].start()
     lax.fori_loop(CUT, BLOCKS, kgrad_step, 0)
@@ -504,6 +502,7 @@
     r1.arrive()
     wb_[...] = wa[x] + wr1[0] + wr1[1] + wr1[2]
     r2.start()
+    wr2[core, y, z] = wb_[y, z]
     lax.fori_loop(5, 8, out_step, 0)
     q1.arrive()
     total = sp[:, :, x, core]
@@ -513,12 +512,7 @@
     q2.start()
     back_sides[1].arrive()
     clear_columns(place, dcv, 1)
-    lax.fori_loop(8, 13, out_step, 0)
-    r2.arrive()
-    wc[...] = wb_[y] + wr2[0] + wr2[1] + wr2[2]
-    r3.start()
-    wr3[core, z] = wc[z]
-    lax.fori_loop(13, BLOCKS, out_step, 0)
+    lax.fori_loop(8, BLOCKS, out_step, 0)
     arrive(*back_nears, *back_fars)
     clear_rows(place, dcv)
     lax.fori_loop(0, BLOCKS, out_rest, 0)
@@ -526,20 +520,22 @@
     put.start()
 
     for stage in stages:
-        if stage not in (r3, q2):
+        if stage not in (r2, q2):
             stage.leave()
     q2.arrive()
     total = sb[y, z]
     for n in range(15):
         total = total + sry[n]
     small_out[...] = total
-    r3.arrive()
+    r2.arrive()
     for kind in range(2):
-        total = wr3[kind, 0] + wr3[kind, 1] + wr3[kind, 2] + wr3[kind, 3]
+        total = wr2[kind, 0, 0]
+        for n in range(1, 16):
+            total = total + wr2[kind, n // 4, n % 4]
         weight_out[kind] = jnp.where(core == 0, total[0:4], total[4:8])
 
     put.wait()
-    r3.leave()
+    r2.leave()
     q2.leave()
 
 
@@ -602,9 +598,9 @@
             half(2 * C, HID), half(C, HID), half(HID, 2 * C), half(2 * C, HID), half(C, HID), vmem(1, HID),
             vmem(C, HID), vmem(C, HID), vmem(8, HID), vmem(K * K, 8, C), vmem(8, C), vmem(8, C),
             vmem(2, 4, 4, 4, 8, C), vmem(4, 4, 4, 8, C), vmem(4, 4, 4, 8, C), vmem(3, 4, 4, 8, C),
-            vmem(4, 4, 8, C), vmem(3, 4, 8, C), vmem(4, 8, C), vmem(2, 4, 8, C),
+            vmem(4, 4, 8, C), vmem(2, 4, 4, 8, C),
             vmem(128, C), vmem(4, 4, 4, 2, 1, C), vmem(7, 4, 4, 1, C), vmem(4, 4, 1, C), vmem(15, 1, C),
-            dma(11), dma(1), dma(27), dma(27),
+            dma(11), dma(1), dma(26), dma(26),
         ],
         compiler_params=pltpu.CompilerParams(
             collective_id=0, has_side_effects=True, vmem_limit_bytes=56 * 2**20

time: 55.3 us -> 54.5 us (0.986)
  Pallas kernels: 51.2 us -> 50.4 us
    pallas_call x1, Pallas kernels: 49.2 us -> 48.4 us  [per_device(): pl.pallas_call(kernel, out_shape=(out(*tile), out(1, C), out(2, 4, C)), i...]
where the time goes in v8:
time: 54.5 us; the launch traced here: 54.3 us
  Pallas kernels  50.4 us (92%)
  between operations  3.88 us (7%)
    pallas_call x1, Pallas kernels, per_device(): pl.pallas_call(kernel, out_shape=(out(*tile), out(1, C), out(2, 4, C)), i...  48.4 us
    pallas_call x1, Pallas kernels, per_device(): pl.pallas_call(deliver, out_shape=(out(*tile), out(K, 1, K), out(1), out(...  2.09 us

profile of v8, /device:TPU:1, one launch (start us, length us, event | category | flops | bytes accessed | tf_op | source)
XLA Modules:
  0.0 54.3 jit_solution(472453734974758522)
XLA Ops:
  3.9 48.4 %shard_map.186 = (f32[2,16,64,128]{3,2,1,0:T(8,128)}, f32[1,128]{1,0:T(1,128)}, f32[2,4,128]{2,1,0:T(4,128)}) custom-call(f32[2,16,64,128]{3,2,1,0:T(8,128)} %feat.1, f32[2,16,64,128]{3,2,1,0:T(8,128)} %cot_hbm.1, f32[7,1,7]{2,1,0:T(1,128)} %bitcast.4, f32[1]{0:T(128)S(6)} %copy.21.cb_in, f32[1]{0:T(128)S(6)} %copy.22.gain_in, f32[1]{0:T(128)S(6)} %copy.23.shift_in, ...), custom_call_target="tpu_custom_call" | custom-call | tf_op jit(solution)/shard_map/pallas_call | solution.py:589
  52.2 2.1 %shard_map.187 = (f32[2,16,64,128]{3,2,1,0:T(8,128)}, f32[7,1,7]{2,1,0:T(1,128)}, f32[1]{0:T(128)}, f32[1]{0:T(128)}, f32[1]{0:T(128)}, /*index=5*/f32[4,128]{1,...) custom-call(f32[2,16,64,128]{3,2,1,0:T(8,128)} %get-tuple-element.23.fg_in, ...), custom_call_target="tpu_custom_call" | custom-call | tf_op jit(solution)/shard_map/pallas_call | solution.py:612

commit v9 on v8

--- a/solution.py
+++ b/solution.py
@@ -23,7 +23,7 @@
 ROWS, COLS = 8, 16
 QUARTER = H // 4
 BLOCKS = B * W // 8
-CUT = BLOCKS // 2 + 1
+CUT = BLOCKS // 2 - 2
 LATE = BLOCKS - 5
 M = 2 * QUARTER * W
 TAPS, CB, GAIN, SHIFT, OB, SCALE, IB = 0, 49, 50, 51, 52, 53, 54

time: 54.5 us -> 54.6 us (level)
  no operation moved by 1% of the time
where the time goes in v9:
time: 54.6 us; the launch traced here: 54.4 us
  Pallas kernels  50.5 us (92%)
  between operations  3.88 us (7%)
    pallas_call x1, Pallas kernels, per_device(): pl.pallas_call(kernel, out_shape=(out(*tile), out(1, C), out(2, 4, C)), i...  48.5 us
    pallas_call x1, Pallas kernels, per_device(): pl.pallas_call(deliver, out_shape=(out(*tile), out(K, 1, K), out(1), out(...  2.09 us

profile of v9, /device:TPU:1, one launch (start us, length us, event | category | flops | bytes accessed | tf_op | source)
XLA Modules:
  0.0 54.4 jit_solution(14305365376451341958)
XLA Ops:
  3.9 48.5 %shard_map.186 = (f32[2,16,64,128]{3,2,1,0:T(8,128)}, f32[1,128]{1,0:T(1,128)}, f32[2,4,128]{2,1,0:T(4,128)}) custom-call(f32[2,16,64,128]{3,2,1,0:T(8,128)} %feat.1, f32[2,16,64,128]{3,2,1,0:T(8,128)} %cot_hbm.1, f32[7,1,7]{2,1,0:T(1,128)} %bitcast.4, f32[1]{0:T(128)S(6)} %copy.21.cb_in, f32[1]{0:T(128)S(6)} %copy.22.gain_in, f32[1]{0:T(128)S(6)} %copy.23.shift_in, ...), custom_call_target="tpu_custom_call" | custom-call | tf_op jit(solution)/shard_map/pallas_call | solution.py:589
  52.3 2.1 %shard_map.187 = (f32[2,16,64,128]{3,2,1,0:T(8,128)}, f32[7,1,7]{2,1,0:T(1,128)}, f32[1]{0:T(128)}, f32[1]{0:T(128)}, f32[1]{0:T(128)}, /*index=5*/f32[4,128]{1,...) custom-call(f32[2,16,64,128]{3,2,1,0:T(8,128)} %get-tuple-element.23.fg_in, ...), custom_call_target="tpu_custom_call" | custom-call | tf_op jit(solution)/shard_map/pallas_call | solution.py:612
